TPU v7x, 512 devices: a whole 4x8x8 slice. The times are simulated.
512 devices in a mesh: rep: 4 (over x), exp: 128 (over z, y, core).
Axes of the slice: x: 4, y: 8, z: 8, core: 2. Of those that a mesh axis runs over, the one named last changes fastest.
Arguments:
- tokens: bfloat16 [3072, 2048], P('exp', 'rep'), may hold values from -6 to 6
- cotangent: bfloat16 [3072, 2048], P('exp', 'rep'), may hold values from -6 to 6
- router_weight: bfloat16 [3072, 8], P('exp'), may hold values from 0.019897461 to 0.5
- expert_ids: int32 [3072, 8], P('exp'), may hold values from 0 to 127, all different within a row; in each aligned block of 24 rows (0 to 23, 24 to 47, ...) at most 2 rows name the same one
- w_gate: bfloat16 [128, 2048, 768], P('exp', 'rep'), may hold values from -0.125 to 0.125
- w_up: bfloat16 [128, 2048, 768], P('exp', 'rep'), may hold values from -0.125 to 0.125
- w_down: bfloat16 [128, 768, 2048], P('exp', None, 'rep'), may hold values from -0.21875 to 0.21875
Outputs:
- mixed: bfloat16 [3072, 2048], P('exp', 'rep')
- token_grad: bfloat16 [3072, 2048], P('exp', 'rep')
- router_grad: bfloat16 [3072, 8], P('exp')
- gate_weight_grad: bfloat16 [128, 2048, 768], P('exp', 'rep')
- up_weight_grad: bfloat16 [128, 2048, 768], P('exp', 'rep')
- down_weight_grad: bfloat16 [128, 768, 2048], P('exp', None, 'rep')
Inputs may be any that keep to these rules, and one draw needn't show every extreme that they name: `expert_ids`: each row names 8 different experts. Among the 24 rows of one index of exp (aligned blocks) no expert is named more than 2 times, a bound that some block reaches.
All inputs are finite; a program needn't handle non-finite values.
Results may differ from a plain program's by a relative error of at most 0.013.
Values may be sent and summed in bfloat16 or wider, within the bound.
No kernel may reach another device: no remote copies, remote signals or barrier semaphores. Data moves between devices by JAX's collectives and lax.ppermute only.
A program may use at most 64 MiB of HBM per device.

v0:
```python
import jax
import jax.numpy as jnp
from jax import lax
from jax.sharding import PartitionSpec as P


def slot_tables(expert_ids, router_weight, experts, capacity):
    expert_range = jnp.arange(experts, dtype=jnp.int32)
    per_token = jnp.sum(
        (expert_ids[:, :, None] == expert_range[None, None, :]).astype(jnp.int32), axis=1
    )
    earlier = jnp.cumsum(per_token, axis=0) - per_token
    ranking = jnp.take_along_axis(earlier, expert_ids, axis=1)
    slot_ids = expert_ids * capacity + ranking
    slot_range = jnp.arange(experts * capacity, dtype=jnp.int32)
    matches = (slot_ids[:, :, None] == slot_range[None, None, :]).astype(jnp.float32)
    placing = jnp.sum(matches, axis=1)
    weighting = jnp.sum(matches * router_weight.astype(jnp.float32)[:, :, None], axis=1)
    return (slot_ids, placing, weighting)


def local(tokens, cotangent, router_weight, expert_ids, w_gate, w_up, w_down):
    experts = lax.axis_size("exp")
    tok_rows, top_count = expert_ids.shape
    capacity = min(tok_rows, max(2, tok_rows * top_count * 3 // (2 * experts)))
    width = tokens.shape[1]
    total = experts * capacity
    slot_ids, placing, weighting = slot_tables(expert_ids, router_weight, experts, capacity)
    place_half = placing.astype(jnp.bfloat16)
    sent_tokens = jnp.dot(place_half.T, tokens, preferred_element_type=jnp.float32).astype(
        jnp.bfloat16
    )
    sent_upstream = jnp.dot(place_half.T, cotangent, preferred_element_type=jnp.float32).astype(
        jnp.bfloat16
    )
    sent_weight = jnp.sum(weighting, axis=0).astype(jnp.bfloat16)
    recv_tokens, recv_upstream, recv_weight = (
        lax.all_to_all(
            sent_tokens.reshape(experts, capacity, width),
            "exp",
            split_axis=0,
            concat_axis=0,
            tiled=True,
        ),
        lax.all_to_all(
            sent_upstream.reshape(experts, capacity, width),
            "exp",
            split_axis=0,
            concat_axis=0,
            tiled=True,
        ),
        lax.all_to_all(
            sent_weight.reshape(experts, capacity), "exp", split_axis=0, concat_axis=0, tiled=True
        ),
    )
    inputs = recv_tokens.reshape(total, width)
    upstream = recv_upstream.reshape(total, width)
    route_weight = recv_weight.reshape(total).astype(jnp.float32)
    gate_mat = w_gate[0]
    up_mat = w_up[0]
    down_mat = w_down[0]
    part_gate = jnp.dot(inputs, gate_mat, preferred_element_type=jnp.float32)
    part_up = jnp.dot(inputs, up_mat, preferred_element_type=jnp.float32)
    gate, upval = lax.psum((part_gate, part_up), "rep")
    active = jax.nn.silu(gate)
    hidden = (active * upval).astype(jnp.bfloat16)
    outputs = jnp.dot(hidden, down_mat, preferred_element_type=jnp.float32).astype(jnp.bfloat16)
    returned = lax.all_to_all(
        outputs.reshape(experts, capacity, width), "exp", split_axis=0, concat_axis=0, tiled=True
    )
    out_delta = (route_weight[:, None] * upstream.astype(jnp.float32)).astype(jnp.bfloat16)
    part_router = jnp.sum(outputs.astype(jnp.float32) * upstream.astype(jnp.float32), axis=1)
    part_hidden = jnp.dot(out_delta, down_mat.T, preferred_element_type=jnp.float32)
    hidden_delta, router_sum = lax.psum((part_hidden, part_router), "rep")
    sigmoid = jax.nn.sigmoid(gate)
    gate_delta = (hidden_delta * upval * sigmoid * (1.0 + gate * (1.0 - sigmoid))).astype(
        jnp.bfloat16
    )
    up_delta = (hidden_delta * active).astype(jnp.bfloat16)
    router_slot = router_sum.astype(jnp.bfloat16)
    down_grad = jnp.dot(hidden.T, out_delta, preferred_element_type=jnp.float32).astype(
        jnp.bfloat16
    )
    gate_grad = jnp.dot(inputs.T, gate_delta, preferred_element_type=jnp.float32).astype(
        jnp.bfloat16
    )
    up_grad = jnp.dot(inputs.T, up_delta, preferred_element_type=jnp.float32).astype(jnp.bfloat16)
    token_delta = (
        jnp.dot(gate_delta, gate_mat.T, preferred_element_type=jnp.float32)
        + jnp.dot(up_delta, up_mat.T, preferred_element_type=jnp.float32)
    ).astype(jnp.bfloat16)
    back_delta, back_router = (
        lax.all_to_all(
            token_delta.reshape(experts, capacity, width),
            "exp",
            split_axis=0,
            concat_axis=0,
            tiled=True,
        ),
        lax.all_to_all(
            router_slot.reshape(experts, capacity), "exp", split_axis=0, concat_axis=0, tiled=True
        ),
    )
    mixed = jnp.dot(
        weighting,
        returned.reshape(total, width).astype(jnp.float32),
        precision=lax.Precision.HIGHEST,
    ).astype(jnp.bfloat16)
    token_grad = jnp.dot(
        place_half, back_delta.reshape(total, width), preferred_element_type=jnp.float32
    ).astype(jnp.bfloat16)
    router_grad = back_router.reshape(total)[slot_ids]
    return (mixed, token_grad, router_grad, gate_grad[None], up_grad[None], down_grad[None])


def solution(mesh):
    return jax.shard_map(
        local,
        mesh=mesh,
        in_specs=(
            P("exp", "rep"),
            P("exp", "rep"),
            P("exp", None),
            P("exp", None),
            P("exp", "rep", None),
            P("exp", "rep", None),
            P("exp", None, "rep"),
        ),
        out_specs=(
            P("exp", "rep"),
            P("exp", "rep"),
            P("exp", None),
            P("exp", "rep", None),
            P("exp", "rep", None),
            P("exp", None, "rep"),
        ),
        check_vma=False,
    )
```

profile of v0, /device:TPU:1, one launch (start us, length us, event | category | flops | bytes accessed | tf_op | source)
XLA Modules:
  0.0 245.7 jit_solution(18139012070512693819)
XLA Ops:
  7.2 0.8 copy.32
  8.3 1.6 gather_fusion.1
  12.3 18.4 %all-to-all-start.2 = ((bf16[128,1,2]{2,1,0:T(2,128)(2,1)}), bf16[128,1,2]{2,1,0:T(2,128)(2,1)S(1)}, u32[]{:S(2)}, u32[]{:S(2)}) async-start(bf16[128,1,2]{2,1,0:T(2,128)(2,1)} %convert_element_type.136), calls=%async_computation.2 | async-start | bytes 131072 | tf_op jit(solution)/shard_map/all_to_all | solution.py:52
  31.0 0.8 reshape.94
  31.8 10.3 %all-to-all-done.2 = bf16[128,1,2]{2,1,0:T(2,128)(2,1)S(1)} async-done(((bf16[128,1,2]{2,1,0:T(2,128)(2,1)}), bf16[128,1,2]{2,1,0:T(2,128)(2,1)S(1)}, u32[]{:S(2)}, u32[]{:S(2)}) %all-to-all-start.2) | async-done | bytes 544 | tf_op jit(solution)/shard_map/all_to_all | solution.py:52
  42.1 5.7 %all-to-all-start.3 = ((bf16[128,2,512]{2,1,0:T(2,128)(2,1)}), bf16[128,2,512]{2,1,0:T(2,128)(2,1)S(1)}, u32[]{:S(2)}, u32[]{:S(2)}) async-start(bf16[128,2,512]{2,1,0:T(2,128)(2,1)} %reshape.94), calls=%async_computation.3 | async-start | bytes 524288 | tf_op jit(solution)/shard_map/all_to_all | solution.py:45
  48.9 14.3 %all-to-all-done.3 = bf16[128,2,512]{2,1,0:T(2,128)(2,1)S(1)} async-done(((bf16[128,2,512]{2,1,0:T(2,128)(2,1)}), bf16[128,2,512]{2,1,0:T(2,128)(2,1)S(1)}, u32[]{:S(2)}, u32[]{:S(2)}) %all-to-all-start.3) | async-done | bytes 262176 | tf_op jit(solution)/shard_map/all_to_all | solution.py:45
  63.2 5.5 %all-to-all-start = ((bf16[128,2,512]{2,1,0:T(2,128)(2,1)}), bf16[128,2,512]{2,1,0:T(2,128)(2,1)S(1)}, u32[]{:S(2)}, u32[]{:S(2)}) async-start(bf16[128,2,512]{2,1,0:T(2,128)(2,1)} %reshape.90), calls=%async_computation | async-start | bytes 524288 | tf_op jit(solution)/shard_map/all_to_all | solution.py:38
  69.3 14.8 %all-to-all-done = bf16[128,2,512]{2,1,0:T(2,128)(2,1)S(1)} async-done(((bf16[128,2,512]{2,1,0:T(2,128)(2,1)}), bf16[128,2,512]{2,1,0:T(2,128)(2,1)S(1)}, u32[]{:S(2)}, u32[]{:S(2)}) %all-to-all-start) | async-done | bytes 262176 | tf_op jit(solution)/shard_map/all_to_all | solution.py:38
  84.3 1.2 fusion.12
  85.5 1.2 fusion.8
  86.8 1.3 fusion.4
  88.1 66.3 %all-reduce.3.cloned.1.call-done = (f32[256,768]{1,0:T(8,128)}, f32[256,768]{1,0:T(8,128)}, f32[256,768]{1,0:T(8,128)}) async-done(((f32[256,768]{1,0:T(8,128)}, f32[256,768]{1,0:T(8,128)}, f32[256,768]{1,0:T(8,128)}), (f32[256,768]{1,0:T(8,128)}, f32[256,768]{1,0:T(8,128)}, f32[256,768]{1,0:T(8,128)})) %all-reduce.3.cloned.1.call-update) | async-done | bytes 2359312 | tf_op jit(solution)/shard_map/psum | solution.py:64
  154.5 2.1 multiply_convert_fusion
  156.5 1.2 fusion.10
  157.7 1.1 multiply_reduce_fusion
  158.8 7.0 %psum.31 = bf16[256]{0:T(256)(128)(2,1)} all-reduce(f32[256]{0:T(256)S(1)} %get-tuple-element.35), channel_id=1, replica_groups=mesh['rep'=4,'exp'=128] {'rep'}, use_global_device_ids=true, to_apply=%region_9.10 | all-reduce | flops 256 | bytes 1536 | tf_op jit(solution)/shard_map/psum | solution.py:74
  165.8 1.4 all_to_all.29
  167.3 16.8 %all-to-all-start.5 = ((bf16[128,1,2]{2,1,0:T(2,128)(2,1)}), bf16[128,1,2]{2,1,0:T(2,128)(2,1)}, u32[]{:S(2)}, u32[]{:S(2)}) async-start(bf16[128,1,2]{2,1,0:T(2,128)(2,1)} %all_to_all.29), calls=%async_computation.5 | async-start | bytes 131072 | tf_op jit(solution)/shard_map/all_to_all | solution.py:100
  184.1 2.1 fusion.3
  186.2 1.8 reshape.95
  188.0 7.2 %all-to-all-done.5 = bf16[128,1,2]{2,1,0:T(2,128)(2,1)} async-done(((bf16[128,1,2]{2,1,0:T(2,128)(2,1)}), bf16[128,1,2]{2,1,0:T(2,128)(2,1)}, u32[]{:S(2)}, u32[]{:S(2)}) %all-to-all-start.5) | async-done | bytes 544 | tf_op jit(solution)/shard_map/all_to_all | solution.py:100
  195.2 6.5 %all-to-all-start.4 = ((bf16[128,2,512]{2,1,0:T(2,128)(2,1)}), bf16[128,2,512]{2,1,0:T(2,128)(2,1)S(1)}, u32[]{:S(2)}, u32[]{:S(2)}) async-start(bf16[128,2,512]{2,1,0:T(2,128)(2,1)} %reshape.95), calls=%async_computation.4 | async-start | bytes 524288 | tf_op jit(solution)/shard_map/all_to_all | solution.py:93
  203.0 1.3 fusion
  204.3 12.7 %all-to-all-done.4 = bf16[128,2,512]{2,1,0:T(2,128)(2,1)S(1)} async-done(((bf16[128,2,512]{2,1,0:T(2,128)(2,1)}), bf16[128,2,512]{2,1,0:T(2,128)(2,1)S(1)}, u32[]{:S(2)}, u32[]{:S(2)}) %all-to-all-start.4) | async-done | bytes 262176 | tf_op jit(solution)/shard_map/all_to_all | solution.py:93
  217.0 5.5 %all-to-all-start.1 = ((bf16[128,2,512]{2,1,0:T(2,128)(2,1)}), bf16[128,2,512]{2,1,0:T(2,128)(2,1)S(1)}, u32[]{:S(2)}, u32[]{:S(2)}) async-start(bf16[128,2,512]{2,1,0:T(2,128)(2,1)} %reshape.92), calls=%async_computation.1 | async-start | bytes 524288 | tf_op jit(solution)/shard_map/all_to_all | solution.py:68
  222.6 1.3 fusion.1
  223.9 1.3 fusion.2
  225.2 1.0 reduce.1
  226.3 1.6 gather_fusion
  229.6 8.4 %all-to-all-done.1 = bf16[128,2,512]{2,1,0:T(2,128)(2,1)S(1)} async-done(((bf16[128,2,512]{2,1,0:T(2,128)(2,1)}), bf16[128,2,512]{2,1,0:T(2,128)(2,1)S(1)}, u32[]{:S(2)}, u32[]{:S(2)}) %all-to-all-start.1) | async-done | bytes 262176 | tf_op jit(solution)/shard_map/all_to_all | solution.py:68
  238.0 0.8 convolution_convert_fusion.7
  (55 shorter events, 7.7 us)
Async XLA Ops:
  7.2 79.6 %copy-start = (bf16[1,768,512]{2,1,0:T(8,128)(2,1)S(1)}, bf16[1,768,512]{2,1,0:T(8,128)(2,1)}, u32[]{:S(2)}) copy-start(bf16[1,768,512]{2,1,0:T(8,128)(2,1)} %param.13) | copy-start | bytes 2359300
  8.3 2.3 copy-start.11
  8.3 22.4 %copy-start.9 = (bf16[24,512]{1,0:T(8,128)(2,1)S(1)}, bf16[24,512]{1,0:T(8,128)(2,1)}, u32[]{:S(2)}) copy-start(bf16[24,512]{1,0:T(8,128)(2,1)} %param.8) | copy-start | bytes 73732
  11.5 36.4 %copy-start.10 = (bf16[24,512]{1,0:T(8,128)(2,1)S(1)}, bf16[24,512]{1,0:T(8,128)(2,1)}, u32[]{:S(2)}) copy-start(bf16[24,512]{1,0:T(8,128)(2,1)} %param.7) | copy-start | bytes 73732
  12.3 29.8 %all-to-all-start.2 = ((bf16[128,1,2]{2,1,0:T(2,128)(2,1)}), bf16[128,1,2]{2,1,0:T(2,128)(2,1)S(1)}, u32[]{:S(2)}, u32[]{:S(2)}) async-start(bf16[128,1,2]{2,1,0:T(2,128)(2,1)} %convert_element_type.136), calls=%async_computation.2 | async-start | bytes 131072 | tf_op jit(solution)/shard_map/all_to_all | solution.py:52
  42.1 26.7 %copy-start.5 = (bf16[128,1,2]{2,1,0:T(2,128)(2,1)}, bf16[128,1,2]{2,1,0:T(2,128)(2,1)S(1)}, u32[]{:S(2)}) copy-start(bf16[128,1,2]{2,1,0:T(2,128)(2,1)S(1)} %all-to-all-done.2) | copy-start | bytes 1540
  42.1 21.1 %all-to-all-start.3 = ((bf16[128,2,512]{2,1,0:T(2,128)(2,1)}), bf16[128,2,512]{2,1,0:T(2,128)(2,1)S(1)}, u32[]{:S(2)}, u32[]{:S(2)}) async-start(bf16[128,2,512]{2,1,0:T(2,128)(2,1)} %reshape.94), calls=%async_computation.3 | async-start | bytes 524288 | tf_op jit(solution)/shard_map/all_to_all | solution.py:45
  63.2 20.9 %all-to-all-start = ((bf16[128,2,512]{2,1,0:T(2,128)(2,1)}), bf16[128,2,512]{2,1,0:T(2,128)(2,1)S(1)}, u32[]{:S(2)}, u32[]{:S(2)}) async-start(bf16[128,2,512]{2,1,0:T(2,128)(2,1)} %reshape.90), calls=%async_computation | async-start | bytes 524288 | tf_op jit(solution)/shard_map/all_to_all | solution.py:38
  68.8 85.7 %all-reduce.3.cloned.1.call-start = ((), (), s32[]{:S(2)}) async-start(), calls=%async_computation.6 | async-start | bytes 4718592 | tf_op jit(solution)/shard_map/psum | solution.py:64
  68.9 15.3 %copy-start.1 = (bf16[1,512,768]{2,1,0:T(8,128)(2,1)S(1)}, bf16[1,512,768]{2,1,0:T(8,128)(2,1)}, u32[]{:S(2)}) copy-start(bf16[1,512,768]{2,1,0:T(8,128)(2,1)} %param.11) | copy-start | bytes 2359300
  84.2 1.3 copy-start.2
  157.7 26.4 %copy-start.3 = (bf16[1,512,768]{2,1,0:T(8,128)(2,1)S(1)}, bf16[1,512,768]{2,1,0:T(8,128)(2,1)}, u32[]{:S(2)}) copy-start(bf16[1,512,768]{2,1,0:T(8,128)(2,1)} %param.12) | copy-start | bytes 2359300
  167.3 28.0 %all-to-all-start.5 = ((bf16[128,1,2]{2,1,0:T(2,128)(2,1)}), bf16[128,1,2]{2,1,0:T(2,128)(2,1)}, u32[]{:S(2)}, u32[]{:S(2)}) async-start(bf16[128,1,2]{2,1,0:T(2,128)(2,1)} %all_to_all.29), calls=%async_computation.5 | async-start | bytes 131072 | tf_op jit(solution)/shard_map/all_to_all | solution.py:100
  186.2 15.5 %copy-start.8 = (s32[24,8]{1,0:T(8,128)S(1)}, s32[24,8]{1,0:T(8,128)}, u32[]{:S(2)}) copy-start(s32[24,8]{1,0:T(8,128)} %get-tuple-element.30) | copy-start | bytes 2308
  186.2 15.7 %copy-start.6 = (bf16[128,1,2]{2,1,0:T(2,128)(2,1)S(1)}, bf16[128,1,2]{2,1,0:T(2,128)(2,1)}, u32[]{:S(2)}) copy-start(bf16[128,1,2]{2,1,0:T(2,128)(2,1)} %copy-done.5) | copy-start | bytes 1540
  186.2 16.0 %copy-start.4 = (bf16[256,512]{1,0:T(8,128)(2,1)S(1)}, bf16[256,512]{1,0:T(8,128)(2,1)}, u32[]{:S(2)}) copy-start(bf16[256,512]{1,0:T(8,128)(2,1)} %get-tuple-element.36) | copy-start | bytes 786436
  195.2 21.8 %all-to-all-start.4 = ((bf16[128,2,512]{2,1,0:T(2,128)(2,1)}), bf16[128,2,512]{2,1,0:T(2,128)(2,1)S(1)}, u32[]{:S(2)}, u32[]{:S(2)}) async-start(bf16[128,2,512]{2,1,0:T(2,128)(2,1)} %reshape.95), calls=%async_computation.4 | async-start | bytes 524288 | tf_op jit(solution)/shard_map/all_to_all | solution.py:93
  217.0 20.9 %all-to-all-start.1 = ((bf16[128,2,512]{2,1,0:T(2,128)(2,1)}), bf16[128,2,512]{2,1,0:T(2,128)(2,1)S(1)}, u32[]{:S(2)}, u32[]{:S(2)}) async-start(bf16[128,2,512]{2,1,0:T(2,128)(2,1)} %reshape.92), calls=%async_computation.1 | async-start | bytes 524288 | tf_op jit(solution)/shard_map/all_to_all | solution.py:68
  227.9 10.1 %copy-start.7 = (f32[24,256]{1,0:T(8,128)S(1)}, f32[24,256]{1,0:T(8,128)}, u32[]{:S(2)}) copy-start(f32[24,256]{1,0:T(8,128)} %get-tuple-element.25) | copy-start | bytes 73732
Sparse Core Ops, SparseCore 0:
  88.2 66.2 all-reduce.2
where the time goes:
time: 246 us
  waiting for transfers between devices  134 us (54%)
  starting transfers between devices  58.6 us (24%)
  between operations  14.3 us (6%)
  matrix products  14.2 us (6%)
  local copies, waits for them, and re-layouts  12.3 us (5%)
  blocking collectives  7.04 us (3%)
  other arithmetic  5.21 us (2%)
    psum x1, waiting for transfers between devices, local(): gate, upval = lax.psum((part_gate, part_up), 'rep')  66.3 us
    all_to_all x1, starting transfers between devices, local(): lax.all_to_all(sent_weight.reshape(experts, capacity), 'exp', split_axis=...  18.4 us
    all_to_all x1, starting transfers between devices, local(): lax.all_to_all(router_slot.reshape(experts, capacity), 'exp', split_axis=...  16.8 us
    all_to_all x1, waiting for transfers between devices, local(): lax.all_to_all(sent_tokens.reshape(experts, capacity, width), 'exp', spli...  14.8 us
    all_to_all x1, waiting for transfers between devices, local(): lax.all_to_all(sent_upstream.reshape(experts, capacity, width), 'exp', sp...  14.3 us
    all_to_all x1, waiting for transfers between devices, local(): lax.all_to_all(token_delta.reshape(experts, capacity, width), 'exp', spli...  12.7 us
    all_to_all x1, waiting for transfers between devices, local(): lax.all_to_all(sent_weight.reshape(experts, capacity), 'exp', split_axis=...  10.3 us
    all_to_all x1, waiting for transfers between devices, local(): lax.all_to_all(outputs.reshape(experts, capacity, width), 'exp', split_ax...  8.38 us
  transfers between devices with their start and end apart: 7, of which 7 were waited for; matrix products, arithmetic and copies ran while one was open for 7% of the time, Pallas kernels for 0%

commit v1 on v0

v1 whole, which is shorter than its diff:
```python
import jax
import jax.numpy as jnp
from jax import lax
from jax.sharding import PartitionSpec as P

BF = jnp.bfloat16
F32 = jnp.float32
LANES = 128


def mm(a, b, dims=(((1,), (0,)), ((), ()))):
    return lax.dot_general(a, b, dims, preferred_element_type=F32)


NT = (((1,), (1,)), ((), ()))
TN = (((0,), (0,)), ((), ()))


def swap(x, axis):
    return lax.all_to_all(x, axis, split_axis=0, concat_axis=0, tiled=True)


def slot_tables(expert_ids, router_weight, experts, capacity):
    rows = expert_ids.shape[0]
    match = expert_ids[:, :, None] == jnp.arange(experts, dtype=jnp.int32)[None, None, :]
    named = jnp.sum(match.astype(F32), axis=1)
    weight = jnp.sum(jnp.where(match, router_weight.astype(F32)[:, :, None], 0.0), axis=1)
    row = jnp.arange(rows)
    before = (row[None, :] < row[:, None]).astype(BF)
    earlier = mm(before, named.astype(BF))
    slot = jnp.arange(capacity, dtype=F32)
    here = (earlier[:, :, None] == slot) & (named[:, :, None] > 0)
    placing = here.astype(BF).reshape(rows, experts * capacity)
    weighting = jnp.where(here, weight[:, :, None], 0.0).astype(BF)
    return match, placing, weighting.reshape(rows, experts * capacity)


def local(tokens, cotangent, router_weight, expert_ids, w_gate, w_up, w_down):
    experts = lax.axis_size("exp")
    reps = lax.axis_size("rep")
    rows, top = expert_ids.shape
    capacity = min(rows, max(2, rows * top * 3 // (2 * experts)))
    width = tokens.shape[1]
    hid = w_gate.shape[2]
    total = experts * capacity
    part = total // reps
    gate_mat, up_mat, down_mat = w_gate[0], w_up[0], w_down[0]

    match, placing, weighting = slot_tables(expert_ids, router_weight, experts, capacity)
    sent = jnp.concatenate(
        [mm(placing, tokens, TN).astype(BF), mm(weighting, cotangent, TN).astype(BF)], axis=1
    )
    recv = swap(sent.reshape(experts, capacity, 2 * width), "exp").reshape(total, 2 * width)
    inputs, out_delta = recv[:, :width], recv[:, width:]

    partial = jnp.concatenate(
        [
            mm(inputs, gate_mat).astype(BF),
            mm(inputs, up_mat).astype(BF),
            mm(out_delta, down_mat, NT).astype(BF),
        ],
        axis=1,
    )
    pieces = swap(partial.reshape(reps, part, 3 * hid), "rep")
    summed = jnp.sum(pieces.astype(F32), axis=0)
    gate, upval, hidden_delta = summed[:, :hid], summed[:, hid : 2 * hid], summed[:, 2 * hid :]
    sigmoid = 1.0 / (1.0 + jnp.exp(-gate))
    active = gate * sigmoid
    hidden = (active * upval).astype(BF)
    gate_delta = (hidden_delta * upval * sigmoid * (1.0 + gate * (1.0 - sigmoid))).astype(BF)
    up_delta = (hidden_delta * active).astype(BF)
    scaled = jnp.sum(hidden.astype(F32) * hidden_delta, axis=1, keepdims=True).astype(BF)
    mine = jnp.concatenate(
        [hidden, gate_delta, up_delta, jnp.broadcast_to(scaled, (part, LANES))], axis=1
    )
    full = swap(jnp.broadcast_to(mine[None], (reps,) + mine.shape), "rep").reshape(total, -1)
    hidden, gate_delta = full[:, :hid], full[:, hid : 2 * hid]
    up_delta, scaled = full[:, 2 * hid : 3 * hid], full[:, 3 * hid :]

    outputs = mm(hidden, down_mat).astype(BF)
    token_delta = (mm(gate_delta, gate_mat, NT) + mm(up_delta, up_mat, NT)).astype(BF)
    back = jnp.concatenate([outputs, token_delta, scaled], axis=1)
    back = swap(back.reshape(experts, capacity, back.shape[1]), "exp").reshape(total, -1)

    down_grad = mm(hidden, out_delta, TN).astype(BF)
    gate_grad = mm(inputs, gate_delta, TN).astype(BF)
    up_grad = mm(inputs, up_delta, TN).astype(BF)

    mixed = mm(weighting, back[:, :width]).astype(BF)
    token_grad = mm(placing, back[:, width : 2 * width]).astype(BF)
    routed = back[:, 2 * width].astype(F32).reshape(1, experts, capacity)
    by_expert = jnp.sum(placing.astype(F32).reshape(rows, experts, capacity) * routed, axis=2)
    router_grad = jnp.sum(jnp.where(match, by_expert[:, None, :], 0.0), axis=2)
    router_grad = (router_grad / router_weight.astype(F32)).astype(BF)
    return (mixed, token_grad, router_grad, gate_grad[None], up_grad[None], down_grad[None])


def solution(mesh):
    return jax.shard_map(
        local,
        mesh=mesh,
        in_specs=(
            P("exp", "rep"),
            P("exp", "rep"),
            P("exp", None),
            P("exp", None),
            P("exp", "rep", None),
            P("exp", "rep", None),
            P("exp", None, "rep"),
        ),
        out_specs=(
            P("exp", "rep"),
            P("exp", "rep"),
            P("exp", None),
            P("exp", "rep", None),
            P("exp", "rep", None),
            P("exp", None, "rep"),
        ),
        check_vma=False,
    )
```

time: 246 us -> 121 us (0.49)
  waiting for transfers between devices: 134 us -> 18.2 us
  blocking collectives: 7.04 us -> 78.4 us
  starting transfers between devices: 58.6 us -> 6.8 us
  between operations: 14.3 us -> 0.91 us
  local copies, waits for them, and re-layouts: 12.3 us -> 5.25 us
  matrix products: 14.2 us -> 9.1 us
  other arithmetic: 5.21 us -> 1.45 us
    all_to_all x0 -> x3, blocking collectives: none -> 78.4 us  [swap(): return lax.all_to_all(x, axis, split_axis=0, concat_axis=0, tiled=True)]
    psum x1 -> x0, waiting for transfers between devices: 66.3 us -> none  [local(): gate, upval = lax.psum((part_gate, part_up), 'rep')]
    all_to_all x6 -> x1, starting transfers between devices: 58.5 us -> 6.8 us  [swap(): return lax.all_to_all(x, axis, split_axis=0, concat_axis=0, tiled=True)]
    all_to_all x6 -> x1, waiting for transfers between devices: 67.7 us -> 18.2 us  [swap(): return lax.all_to_all(x, axis, split_axis=0, concat_axis=0, tiled=True)]
    psum x1 -> x0, blocking collectives: 7.04 us -> none  [local(): hidden_delta, router_sum = lax.psum((part_hidden, part_router), 'rep')]
    dot_general x13 -> x14, matrix products: 14.2 us -> 9.1 us  [mm(): return lax.dot_general(a, b, dims, preferred_element_type=F32)]
    gather x5 -> x0, local copies, waits for them, and re-layouts: 3.38 us -> none  [the longest x3 1.73 us: slot_tables(): ranking = jnp.take_along_axis(earlier, expert_ids, axis=1)]
    reshape x8 -> x4, local copies, waits for them, and re-layouts: 4.66 us -> 1.66 us  [the longest x1 1.03 us: local(): back.reshape(experts, capacity, back.shape[1])]
  transfers between devices with their start and end apart: 7 -> 1, of which waited for: 7 -> 1; matrix products, arithmetic and copies ran while one was open for 7% -> 3% of each run, Pallas kernels for 0% -> 0%
where the time goes in v1:
time: 121 us; the launch traced here: 120 us
  blocking collectives  78.4 us (65%)
  waiting for transfers between devices  18.2 us (15%)
  matrix products  9.1 us (8%)
  starting transfers between devices  6.8 us (6%)
  local copies, waits for them, and re-layouts  5.25 us (4%)
  other arithmetic  1.45 us (1%)
    all_to_all x3, blocking collectives, swap(): return lax.all_to_all(x, axis, split_axis=0, concat_axis=0, tiled=True)  78.4 us
    all_to_all x1, waiting for transfers between devices, swap(): return lax.all_to_all(x, axis, split_axis=0, concat_axis=0, tiled=True)  18.2 us
    dot_general x14, matrix products, mm(): return lax.dot_general(a, b, dims, preferred_element_type=F32)  9.1 us
    all_to_all x1, starting transfers between devices, swap(): return lax.all_to_all(x, axis, split_axis=0, concat_axis=0, tiled=True)  6.8 us
    unnamed x11, local copies, waits for them, and re-layouts  2.61 us
  transfers between devices with their start and end apart: 1, of which 1 were waited for; matrix products, arithmetic and copies ran while one was open for 3% of the time, Pallas kernels for 0%

profile of v1, /device:TPU:1, one launch (start us, length us, event | category | flops | bytes accessed | tf_op | source)
XLA Modules:
  0.0 120.1 jit_solution(7629691239830609374)
XLA Ops:
  0.7 0.8 copy.29
  1.5 0.8 copy.26
  2.4 0.2 fusion.26
  3.4 0.9 convolution_convert_fusion.7
  4.4 0.2 convolution_convert_fusion.6
  4.6 0.2 reshape.70
  4.9 38.9 %all_to_all.20 = bf16[128,2,1024]{2,1,0:T(2,128)(2,1)S(1)} all-to-all(bf16[128,2,1024]{2,1,0:T(2,128)(2,1)S(1)} %reshape.70), channel_id=1, replica_groups=mesh['rep'=4,'exp'=128] {'exp'}, dimensions={0} | all-to-all | bytes 1048576 | tf_op jit(solution)/shard_map/all_to_all | solution.py:20
  43.8 0.2 reshape.71
  44.0 0.4 convolution_convert_fusion.4
  44.4 0.4 convolution_convert_fusion.3
  44.8 0.3 copy-done.1
  45.2 0.4 convolution_convert_fusion.5
  45.6 20.5 %all_to_all.21 = bf16[4,64,2304]{2,1,0:T(8,128)(2,1)S(1)} all-to-all(bf16[4,64,2304]{2,1,0:T(8,128)(2,1)S(1)} %bitcast.38), channel_id=1, replica_groups=mesh['rep'=4,'exp'=128] {'rep'}, dimensions={0} | all-to-all | bytes 2359296 | tf_op jit(solution)/shard_map/all_to_all | solution.py:20
  66.1 0.2 convert_reduce_fusion
  66.3 0.2 multiply_convert_fusion.1
  66.7 18.9 %all_to_all.22 = bf16[4,64,2432]{2,1,0:T(8,128)(2,1)S(1)} all-to-all(bf16[4,64,2432]{2,1,0:T(8,128)(2,1)S(1)} %broadcast_in_dim.73), channel_id=1, replica_groups=mesh['rep'=4,'exp'=128] {'rep'}, dimensions={0} | all-to-all | bytes 2490368 | tf_op jit(solution)/shard_map/all_to_all | solution.py:20
  85.7 0.4 convolution_convert_fusion.8
  86.1 0.4 fusion.8
  86.5 0.4 fusion.3
  86.9 1.0 reshape.74
  88.0 6.8 %all-to-all-start.3 = ((bf16[128,2,1152]{2,1,0:T(2,128)(2,1)}), bf16[128,2,1152]{2,1,0:T(2,128)(2,1)S(1)}, u32[]{:S(2)}, u32[]{:S(2)}) async-start(bf16[128,2,1152]{2,1,0:T(2,128)(2,1)} %reshape.74), calls=%async_computation.3 | async-start | bytes 1179648 | tf_op jit(solution)/shard_map/all_to_all | solution.py:20
  94.8 1.3 %fusion = bf16[1,512,768]{2,1,0:T(8,128)(2,1)} fusion(bf16[256,2432]{1,0:T(8,128)(2,1)S(1)} %bitcast.35, bf16[256,1024]{1,0:T(8,128)(2,1)S(1)} %reshape.71), kind=kOutput, calls=%fused_computation.4 | convolution fusion | flops 201719808 | bytes 1441792 | tf_op jit(solution)/shard_map/dot_general | solution.py:12
  96.1 1.3 %fusion.1 = bf16[1,512,768]{2,1,0:T(8,128)(2,1)} fusion(bf16[256,2432]{1,0:T(8,128)(2,1)S(1)} %bitcast.36, bf16[256,1024]{1,0:T(8,128)(2,1)S(1)} %reshape.71), kind=kOutput, calls=%fused_computation.5 | convolution fusion | flops 201719808 | bytes 1441792 | tf_op jit(solution)/shard_map/dot_general | solution.py:12
  97.4 1.3 %fusion.2 = bf16[1,768,512]{2,1,0:T(8,128)(2,1)} fusion(bf16[256,2432]{1,0:T(8,128)(2,1)S(1)} %bitcast.37, bf16[256,1024]{1,0:T(8,128)(2,1)S(1)} %reshape.71), kind=kOutput, calls=%fused_computation.6 | convolution fusion | flops 201719808 | bytes 1441792 | tf_op jit(solution)/shard_map/dot_general | solution.py:12
  98.6 18.2 %all-to-all-done.3 = bf16[128,2,1152]{2,1,0:T(2,128)(2,1)S(1)} async-done(((bf16[128,2,1152]{2,1,0:T(2,128)(2,1)}), bf16[128,2,1152]{2,1,0:T(2,128)(2,1)S(1)}, u32[]{:S(2)}, u32[]{:S(2)}) %all-to-all-start.3) | async-done | bytes 589856 | tf_op jit(solution)/shard_map/all_to_all | solution.py:20
  116.8 0.2 reshape.75
  117.1 0.8 convolution_convert_fusion.10
  117.9 0.8 convolution_convert_fusion.9
  118.8 0.1 reshape.76
  118.9 0.3 multiply_reduce_fusion.1
  119.3 0.2 select_reduce_fusion
  119.5 0.7 copy.32
  (29 shorter events, 1.4 us)
Async XLA Ops:
  0.6 43.8 %copy-start = (bf16[1,768,512]{2,1,0:T(8,128)(2,1)S(1)}, bf16[1,768,512]{2,1,0:T(8,128)(2,1)}, u32[]{:S(2)}) copy-start(bf16[1,768,512]{2,1,0:T(8,128)(2,1)} %param.13) | copy-start | bytes 2359300
  0.6 3.7 %copy-start.3 = (bf16[24,512]{1,0:T(8,128)(2,1)S(1)}, bf16[24,512]{1,0:T(8,128)(2,1)}, u32[]{:S(2)}) copy-start(bf16[24,512]{1,0:T(8,128)(2,1)} %param.8) | copy-start | bytes 73732
  4.9 39.2 %copy-start.2 = (bf16[1,512,768]{2,1,0:T(8,128)(2,1)S(1)}, bf16[1,512,768]{2,1,0:T(8,128)(2,1)}, u32[]{:S(2)}) copy-start(bf16[1,512,768]{2,1,0:T(8,128)(2,1)} %param.12) | copy-start | bytes 2359300
  44.0 1.1 copy-start.1
  88.0 28.9 %all-to-all-start.3 = ((bf16[128,2,1152]{2,1,0:T(2,128)(2,1)}), bf16[128,2,1152]{2,1,0:T(2,128)(2,1)S(1)}, u32[]{:S(2)}, u32[]{:S(2)}) async-start(bf16[128,2,1152]{2,1,0:T(2,128)(2,1)} %reshape.74), calls=%async_computation.3 | async-start | bytes 1179648 | tf_op jit(solution)/shard_map/all_to_all | solution.py:20

commit v2 on v1

--- a/solution.py
+++ b/solution.py
@@ -51,18 +51,31 @@
         [mm(placing, tokens, TN).astype(BF), mm(weighting, cotangent, TN).astype(BF)], axis=1
     )
     recv = swap(sent.reshape(experts, capacity, 2 * width), "exp").reshape(total, 2 * width)
-    inputs, out_delta = recv[:, :width], recv[:, width:]
 
-    partial = jnp.concatenate(
-        [
-            mm(inputs, gate_mat).astype(BF),
-            mm(inputs, up_mat).astype(BF),
-            mm(out_delta, down_mat, NT).astype(BF),
-        ],
-        axis=1,
-    )
-    pieces = swap(partial.reshape(reps, part, 3 * hid), "rep")
-    summed = jnp.sum(pieces.astype(F32), axis=0)
+    me = lax.axis_index("rep")
+
+    def rows_of(array, owner):
+        return lax.dynamic_slice_in_dim(array, owner * part, part, 0)
+
+    def to_peer(array, step):
+        return lax.ppermute(array, "rep", [(i, (i + step) % reps) for i in range(reps)])
+
+    def partial(owner):
+        rows_in = rows_of(recv, owner)
+        return jnp.concatenate(
+            [
+                mm(rows_in[:, :width], gate_mat),
+                mm(rows_in[:, :width], up_mat),
+                mm(rows_in[:, width:], down_mat, NT),
+            ],
+            axis=1,
+        )
+
+    steps = [2, 1, 3]
+    arrived = [to_peer(partial((me + d) % reps).astype(BF), d) for d in steps]
+    summed = partial(me)
+    for piece in arrived:
+        summed = summed + piece.astype(F32)
     gate, upval, hidden_delta = summed[:, :hid], summed[:, hid : 2 * hid], summed[:, 2 * hid :]
     sigmoid = 1.0 / (1.0 + jnp.exp(-gate))
     active = gate * sigmoid
@@ -73,18 +86,25 @@
     mine = jnp.concatenate(
         [hidden, gate_delta, up_delta, jnp.broadcast_to(scaled, (part, LANES))], axis=1
     )
-    full = swap(jnp.broadcast_to(mine[None], (reps,) + mine.shape), "rep").reshape(total, -1)
-    hidden, gate_delta = full[:, :hid], full[:, hid : 2 * hid]
-    up_delta, scaled = full[:, 2 * hid : 3 * hid], full[:, 3 * hid :]
+    owners = [me] + [(me - d) % reps for d in steps]
+    pieces = [mine] + [to_peer(mine, d) for d in steps]
 
-    outputs = mm(hidden, down_mat).astype(BF)
-    token_delta = (mm(gate_delta, gate_mat, NT) + mm(up_delta, up_mat, NT)).astype(BF)
-    back = jnp.concatenate([outputs, token_delta, scaled], axis=1)
-    back = swap(back.reshape(experts, capacity, back.shape[1]), "exp").reshape(total, -1)
+    back = jnp.zeros((experts, capacity, 2 * width + LANES), BF)
+    for owner, piece in zip(owners, pieces):
+        outputs = mm(piece[:, :hid], down_mat).astype(BF)
+        token_delta = mm(piece[:, hid : 2 * hid], gate_mat, NT)
+        token_delta = (token_delta + mm(piece[:, 2 * hid : 3 * hid], up_mat, NT)).astype(BF)
+        block = jnp.concatenate([outputs, token_delta, piece[:, 3 * hid :]], axis=1)
+        block = block.reshape(part // capacity, capacity, 2 * width + LANES)
+        back = lax.dynamic_update_slice_in_dim(back, block, owner * (part // capacity), 0)
+    back = swap(back, "exp").reshape(total, -1)
 
-    down_grad = mm(hidden, out_delta, TN).astype(BF)
-    gate_grad = mm(inputs, gate_delta, TN).astype(BF)
-    up_grad = mm(inputs, up_delta, TN).astype(BF)
+    full = jnp.concatenate(pieces, axis=0)
+    recv = jnp.concatenate([rows_of(recv, owner) for owner in owners], axis=0)
+    inputs, out_delta = recv[:, :width], recv[:, width:]
+    down_grad = mm(full[:, :hid], out_delta, TN).astype(BF)
+    gate_grad = mm(inputs, full[:, hid : 2 * hid], TN).astype(BF)
+    up_grad = mm(inputs, full[:, 2 * hid : 3 * hid], TN).astype(BF)
 
     mixed = mm(weighting, back[:, :width]).astype(BF)
     token_grad = mm(placing, back[:, width : 2 * width]).astype(BF)

time: 121 us -> 144 us (1.19)
  blocking collectives: 78.4 us -> 0 us
  starting transfers between devices: 6.8 us -> 50.9 us
  waiting for transfers between devices: 18.2 us -> 45.7 us
  matrix products: 9.1 us -> 25.1 us
  local copies, waits for them, and re-layouts: 5.25 us -> 15.2 us
  other arithmetic: 1.45 us -> 4.99 us
    all_to_all x3 -> x0, blocking collectives: 78.4 us -> none  [swap(): return lax.all_to_all(x, axis, split_axis=0, concat_axis=0, tiled=True)]
    all_to_all x1 -> x2, starting transfers between devices: 6.8 us -> 30.5 us  [swap(): return lax.all_to_all(x, axis, split_axis=0, concat_axis=0, tiled=True)]
    ppermute x0 -> x6, starting transfers between devices: none -> 20.5 us  [to_peer(): lax.ppermute(array, 'rep', [(i, (i + step) % reps) for i in range(reps)])]
    all_to_all x1 -> x2, waiting for transfers between devices: 18.2 us -> 35.6 us  [swap(): return lax.all_to_all(x, axis, split_axis=0, concat_axis=0, tiled=True)]
    dot_general x14 -> x32, matrix products: 9.1 us -> 25.1 us  [mm(): return lax.dot_general(a, b, dims, preferred_element_type=F32)]
    ppermute x0 -> x6, waiting for transfers between devices: none -> 10.1 us  [to_peer(): lax.ppermute(array, 'rep', [(i, (i + step) % reps) for i in range(reps)])]
    dynamic_update_slice x0 -> x4, local copies, waits for them, and re-layouts: none -> 3.04 us  [local(): lax.dynamic_update_slice_in_dim(back, block, owner * (part // capacity), 0)]
    concatenate x2 -> x8, other arithmetic: 0.13 us -> 2.98 us  [the longest x4 2.88 us: local(): block = jnp.concatenate([outputs, token_delta, piece[:, 3 * hid:]], axis=1)]
  transfers between devices with their start and end apart: 1 -> 8, of which waited for: 1 -> 6; matrix products, arithmetic and copies ran while one was open for 3% -> 18% of each run, Pallas kernels for 0% -> 0%
where the time goes in v2:
time: 144 us; the launch traced here: 143 us
  starting transfers between devices  50.9 us (35%)
  waiting for transfers between devices  45.7 us (32%)
  matrix products  25.1 us (17%)
  local copies, waits for them, and re-layouts  15.2 us (11%)
  other arithmetic  4.99 us (3%)
    all_to_all x2, waiting for transfers between devices, swap(): return lax.all_to_all(x, axis, split_axis=0, concat_axis=0, tiled=True)  35.6 us
    all_to_all x2, starting transfers between devices, swap(): return lax.all_to_all(x, axis, split_axis=0, concat_axis=0, tiled=True)  30.5 us
    dot_general x32, matrix products, mm(): return lax.dot_general(a, b, dims, preferred_element_type=F32)  25.1 us
    ppermute x6, starting transfers between devices, to_peer(): lax.ppermute(array, 'rep', [(i, (i + step) % reps) for i in range(reps)])  20.5 us
    ppermute x6, waiting for transfers between devices, to_peer(): lax.ppermute(array, 'rep', [(i, (i + step) % reps) for i in range(reps)])  10.1 us
    reshape x4, local copies, waits for them, and re-layouts, local(): block = block.reshape(part // capacity, capacity, 2 * width + LANES)  3.62 us
    dynamic_update_slice x4, local copies, waits for them, and re-layouts, local(): lax.dynamic_update_slice_in_dim(back, block, owner * (part // capacity), 0)  3.04 us
    unnamed x19, local copies, waits for them, and re-layouts  2.9 us
  transfers between devices with their start and end apart: 8, of which 6 were waited for; matrix products, arithmetic and copies ran while one was open for 18% of the time, Pallas kernels for 0%

profile of v2, /device:TPU:1, one launch (start us, length us, event | category | flops | bytes accessed | tf_op | source)
XLA Modules:
  0.0 143.1 jit_solution(10397280143663508189)
XLA Ops:
  0.7 0.8 copy.32
  4.5 1.0 reshape.72
  5.5 18.4 %all-to-all-start = ((bf16[128,2,1024]{2,1,0:T(2,128)(2,1)}), bf16[128,2,1024]{2,1,0:T(2,128)(2,1)S(1)}, u32[]{:S(2)}, u32[]{:S(2)}) async-start(bf16[128,2,1024]{2,1,0:T(2,128)(2,1)} %reshape.72), calls=%async_computation | async-start | bytes 1048576 | tf_op jit(solution)/shard_map/all_to_all | solution.py:20
  24.1 20.4 %all-to-all-done = bf16[128,2,1024]{2,1,0:T(2,128)(2,1)S(1)} async-done(((bf16[128,2,1024]{2,1,0:T(2,128)(2,1)}), bf16[128,2,1024]{2,1,0:T(2,128)(2,1)S(1)}, u32[]{:S(2)}, u32[]{:S(2)}) %all-to-all-start) | async-done | bytes 524320 | tf_op jit(solution)/shard_map/all_to_all | solution.py:20
  47.8 3.1 %collective-permute-start.1 = (bf16[64,2304]{1,0:T(8,128)(2,1)S(1)}, bf16[64,2304]{1,0:T(8,128)(2,1)S(1)}, u32[]{:S(2)}, u32[]{:S(2)}) collective-permute-start(bf16[64,2304]{1,0:T(8,128)(2,1)S(1)} %pad_maximum_fusion.16), channel_id=1, source_target_pairs={{0,128},{128,256},{256,384},{384,0},{1,129},{129,257},{257,385},{3... | collective-permute-start | bytes 884744 | tf_op jit(solution)/shard_map/ppermute | solution.py:61
  51.0 4.4 %collective-permute-start = (bf16[64,2304]{1,0:T(8,128)(2,1)S(1)}, bf16[64,2304]{1,0:T(8,128)(2,1)S(1)}, u32[]{:S(2)}, u32[]{:S(2)}) collective-permute-start(bf16[64,2304]{1,0:T(8,128)(2,1)S(1)} %pad_maximum_fusion.15), channel_id=1, source_target_pairs={{0,256},{128,384},{256,0},{384,128},{1,257},{129,385},{257,1},{385... | collective-permute-start | bytes 884744 | tf_op jit(solution)/shard_map/ppermute | solution.py:61
  55.4 3.1 %collective-permute-start.2 = (bf16[64,2304]{1,0:T(8,128)(2,1)S(1)}, bf16[64,2304]{1,0:T(8,128)(2,1)S(1)}, u32[]{:S(2)}, u32[]{:S(2)}) collective-permute-start(bf16[64,2304]{1,0:T(8,128)(2,1)S(1)} %pad_maximum_fusion.17), channel_id=1, source_target_pairs={{0,384},{128,0},{256,128},{384,256},{1,385},{129,1},{257,129},{385... | collective-permute-start | bytes 884744 | tf_op jit(solution)/shard_map/ppermute | solution.py:61
  59.0 0.9 collective-permute-done.1
  59.9 7.3 %collective-permute-done = bf16[64,2304]{1,0:T(8,128)(2,1)S(1)} collective-permute-done((bf16[64,2304]{1,0:T(8,128)(2,1)S(1)}, bf16[64,2304]{1,0:T(8,128)(2,1)S(1)}, u32[]{:S(2)}, u32[]{:S(2)}) %collective-permute-start) | collective-permute-done | bytes 294944 | tf_op jit(solution)/shard_map/ppermute | solution.py:61
  67.2 1.3 collective-permute-done.2
  70.3 4.5 %collective-permute-start.5 = (bf16[64,2432]{1,0:T(8,128)(2,1)}, bf16[64,2432]{1,0:T(8,128)(2,1)}, u32[]{:S(2)}, u32[]{:S(2)}) collective-permute-start(bf16[64,2432]{1,0:T(8,128)(2,1)} %pad_maximum_fusion.14), channel_id=1, source_target_pairs={{0,384},{128,0},{256,128},{384,256},{1,385},{129,1},{257,129},{385... | collective-permute-start | bytes 933896 | tf_op jit(solution)/shard_map/ppermute | solution.py:61
  74.8 1.9 %collective-permute-start.4 = (bf16[64,2432]{1,0:T(8,128)(2,1)}, bf16[64,2432]{1,0:T(8,128)(2,1)}, u32[]{:S(2)}, u32[]{:S(2)}) collective-permute-start(bf16[64,2432]{1,0:T(8,128)(2,1)} %pad_maximum_fusion.14), channel_id=1, source_target_pairs={{0,128},{128,256},{256,384},{384,0},{1,129},{129,257},{257,385},{3... | collective-permute-start | bytes 933896 | tf_op jit(solution)/shard_map/ppermute | solution.py:61
  76.8 3.5 %collective-permute-start.3 = (bf16[64,2432]{1,0:T(8,128)(2,1)}, bf16[64,2432]{1,0:T(8,128)(2,1)}, u32[]{:S(2)}, u32[]{:S(2)}) collective-permute-start(bf16[64,2432]{1,0:T(8,128)(2,1)} %pad_maximum_fusion.14), channel_id=1, source_target_pairs={{0,256},{128,384},{256,0},{384,128},{1,257},{129,385},{257,1},{385... | collective-permute-start | bytes 933896 | tf_op jit(solution)/shard_map/ppermute | solution.py:61
  81.3 1.0 reshape.74
  82.3 1.1 broadcast_in_dim.69
  84.1 1.1 convolution_convert_fusion.14
  86.0 1.2 fusion.16
  87.8 1.8 %convolution_convert_fusion.15 = bf16[64,512]{1,0:T(8,128)(2,1)} fusion(bf16[1,768,512]{2,1,0:T(8,128)(2,1)S(1)} %copy-done, bf16[64,2432]{1,0:T(8,128)(2,1)} %collective-permute-done.4), kind=kOutput, calls=%fused_computation.26 | convolution fusion | flops 50364416 | bytes 950272 | tf_op jit(solution)/shard_map/dot_general | solution.py:12
  89.6 1.2 fusion.18
  90.8 1.3 fusion.6
  92.1 1.3 fusion.5
  94.0 1.0 reshape.77
  95.7 1.5 %pad_maximum_fusion.20 = bf16[64,1152]{1,0:T(8,128)(2,1)} fusion(bf16[64,128]{1,0:T(8,128)(2,1)S(1)} %slice.138, bf16[64,512]{1,0:T(8,128)(2,1)S(1)} %fusion.5, bf16[64,512]{1,0:T(8,128)(2,1)} %convolution_convert_fusion.15), kind=kLoop, calls=%fused_computation.118 | loop fusion | flops 442368 | bytes 294912 | tf_op jit(solution)/shard_map/concatenate | solution.py:97
  97.2 1.6 %reshape.76 = bf16[32,2,1152]{2,1,0:T(2,128)(2,1)} reshape(bf16[64,1152]{1,0:T(8,128)(2,1)} %pad_maximum_fusion.20) | data formatting | bytes 294912 | tf_op jit(solution)/shard_map/reshape | solution.py:98
  99.6 1.1 convolution_convert_fusion.16
  100.7 1.3 fusion.20
  102.0 1.3 fusion.4
  105.7 12.1 %all-to-all-start.1 = ((bf16[128,2,1152]{2,1,0:T(2,128)(2,1)}), bf16[128,2,1152]{2,1,0:T(2,128)(2,1)S(1)}, u32[]{:S(2)}, u32[]{:S(2)}) async-start(bf16[128,2,1152]{2,1,0:T(2,128)(2,1)} %constant_dynamic-update-slice_fusion), calls=%async_computation.1 | async-start | bytes 1179648 | tf_op jit(solution)/shard_map/all_to_all | solution.py:20
  117.9 2.3 %fusion.1 = bf16[1,512,768]{2,1,0:T(8,128)(2,1)} fusion(bf16[64,2432]{1,0:T(8,128)(2,1)} %collective-permute-done.5, bf16[64,2432]{1,0:T(8,128)(2,1)} %collective-permute-done.4, bf16[64,2432]{1,0:T(8,128)(2,1)} %collective-permute-done.3, bf16[64,128]{1,0:T(8,128)(2,1)S(1)} %broadcast_in_dim.70, bf16[64,768]{1,0:T(8,128)(2,1)S(1)} %get-tuple-element.16, ...), kind=kOutput, calls=%fused_computation.4 | convolution fusion | flops 204472320 | bytes 2293760 | tf_op jit(solution)/shard_map/dot_general | solution.py:12
  120.1 2.3 %fusion = bf16[1,512,768]{2,1,0:T(8,128)(2,1)} fusion(bf16[64,2432]{1,0:T(8,128)(2,1)} %collective-permute-done.5, bf16[64,2432]{1,0:T(8,128)(2,1)} %collective-permute-done.4, bf16[64,2432]{1,0:T(8,128)(2,1)} %collective-permute-done.3, bf16[64,128]{1,0:T(8,128)(2,1)S(1)} %broadcast_in_dim.70, bf16[64,768]{1,0:T(8,128)(2,1)S(1)} %get-tuple-element.16, ...), kind=kOutput, calls=%fused_computation.3 | convolution fusion | flops 204472320 | bytes 2293760 | tf_op jit(solution)/shard_map/dot_general | solution.py:12
  122.4 2.3 %fusion.2 = bf16[1,768,512]{2,1,0:T(8,128)(2,1)} fusion(bf16[64,2432]{1,0:T(8,128)(2,1)} %collective-permute-done.5, bf16[64,2432]{1,0:T(8,128)(2,1)} %collective-permute-done.4, bf16[64,2432]{1,0:T(8,128)(2,1)} %collective-permute-done.3, bf16[64,128]{1,0:T(8,128)(2,1)S(1)} %broadcast_in_dim.70, bf16[64,768]{1,0:T(8,128)(2,1)S(1)} %get-tuple-element.16, ...), kind=kOutput, calls=%fused_computation.5 | convolution fusion | flops 204472320 | bytes 2293760 | tf_op jit(solution)/shard_map/dot_general | solution.py:12
  124.7 15.1 %all-to-all-done.1 = bf16[128,2,1152]{2,1,0:T(2,128)(2,1)S(1)} async-done(((bf16[128,2,1152]{2,1,0:T(2,128)(2,1)}), bf16[128,2,1152]{2,1,0:T(2,128)(2,1)S(1)}, u32[]{:S(2)}, u32[]{:S(2)}) %all-to-all-start.1) | async-done | bytes 589856 | tf_op jit(solution)/shard_map/all_to_all | solution.py:20
  (82 shorter events, 19.4 us)
Async XLA Ops:
  0.6 45.2 %copy-start = (bf16[1,768,512]{2,1,0:T(8,128)(2,1)S(1)}, bf16[1,768,512]{2,1,0:T(8,128)(2,1)}, u32[]{:S(2)}) copy-start(bf16[1,768,512]{2,1,0:T(8,128)(2,1)} %param.13) | copy-start | bytes 2359300
  0.6 2.7 %copy-start.6 = (bf16[24,512]{1,0:T(8,128)(2,1)S(1)}, bf16[24,512]{1,0:T(8,128)(2,1)}, u32[]{:S(2)}) copy-start(bf16[24,512]{1,0:T(8,128)(2,1)} %param.7) | copy-start | bytes 73732
  0.7 3.6 %copy-start.7 = (bf16[24,512]{1,0:T(8,128)(2,1)S(1)}, bf16[24,512]{1,0:T(8,128)(2,1)}, u32[]{:S(2)}) copy-start(bf16[24,512]{1,0:T(8,128)(2,1)} %param.8) | copy-start | bytes 73732
  3.6 0.6 copy-start.4
  5.5 39.0 %all-to-all-start = ((bf16[128,2,1024]{2,1,0:T(2,128)(2,1)}), bf16[128,2,1024]{2,1,0:T(2,128)(2,1)S(1)}, u32[]{:S(2)}, u32[]{:S(2)}) async-start(bf16[128,2,1024]{2,1,0:T(2,128)(2,1)} %reshape.72), calls=%async_computation | async-start | bytes 1048576 | tf_op jit(solution)/shard_map/all_to_all | solution.py:20
  24.0 20.8 %copy-start.1 = (bf16[1,512,768]{2,1,0:T(8,128)(2,1)S(1)}, bf16[1,512,768]{2,1,0:T(8,128)(2,1)}, u32[]{:S(2)}) copy-start(bf16[1,512,768]{2,1,0:T(8,128)(2,1)} %param.12) | copy-start | bytes 2359300
  24.1 20.9 %copy-start.2 = (bf16[1,512,768]{2,1,0:T(8,128)(2,1)S(1)}, bf16[1,512,768]{2,1,0:T(8,128)(2,1)}, u32[]{:S(2)}) copy-start(bf16[1,512,768]{2,1,0:T(8,128)(2,1)} %param.11) | copy-start | bytes 2359300
  47.8 12.1 %collective-permute-start.1 = (bf16[64,2304]{1,0:T(8,128)(2,1)S(1)}, bf16[64,2304]{1,0:T(8,128)(2,1)S(1)}, u32[]{:S(2)}, u32[]{:S(2)}) collective-permute-start(bf16[64,2304]{1,0:T(8,128)(2,1)S(1)} %pad_maximum_fusion.16), channel_id=1, source_target_pairs={{0,128},{128,256},{256,384},{384,0},{1,129},{129,257},{257,385},{3... | collective-permute-start | bytes 884744 | tf_op jit(solution)/shard_map/ppermute | solution.py:61
  51.0 16.2 %collective-permute-start = (bf16[64,2304]{1,0:T(8,128)(2,1)S(1)}, bf16[64,2304]{1,0:T(8,128)(2,1)S(1)}, u32[]{:S(2)}, u32[]{:S(2)}) collective-permute-start(bf16[64,2304]{1,0:T(8,128)(2,1)S(1)} %pad_maximum_fusion.15), channel_id=1, source_target_pairs={{0,256},{128,384},{256,0},{384,128},{1,257},{129,385},{257,1},{385... | collective-permute-start | bytes 884744 | tf_op jit(solution)/shard_map/ppermute | solution.py:61
  55.4 13.1 %collective-permute-start.2 = (bf16[64,2304]{1,0:T(8,128)(2,1)S(1)}, bf16[64,2304]{1,0:T(8,128)(2,1)S(1)}, u32[]{:S(2)}, u32[]{:S(2)}) collective-permute-start(bf16[64,2304]{1,0:T(8,128)(2,1)S(1)} %pad_maximum_fusion.17), channel_id=1, source_target_pairs={{0,384},{128,0},{256,128},{384,256},{1,385},{129,1},{257,129},{385... | collective-permute-start | bytes 884744 | tf_op jit(solution)/shard_map/ppermute | solution.py:61
  70.3 13.8 %collective-permute-start.5 = (bf16[64,2432]{1,0:T(8,128)(2,1)}, bf16[64,2432]{1,0:T(8,128)(2,1)}, u32[]{:S(2)}, u32[]{:S(2)}) collective-permute-start(bf16[64,2432]{1,0:T(8,128)(2,1)} %pad_maximum_fusion.14), channel_id=1, source_target_pairs={{0,384},{128,0},{256,128},{384,256},{1,385},{129,1},{257,129},{385... | collective-permute-start | bytes 933896 | tf_op jit(solution)/shard_map/ppermute | solution.py:61
  74.8 13.0 %collective-permute-start.4 = (bf16[64,2432]{1,0:T(8,128)(2,1)}, bf16[64,2432]{1,0:T(8,128)(2,1)}, u32[]{:S(2)}, u32[]{:S(2)}) collective-permute-start(bf16[64,2432]{1,0:T(8,128)(2,1)} %pad_maximum_fusion.14), channel_id=1, source_target_pairs={{0,128},{128,256},{256,384},{384,0},{1,129},{129,257},{257,385},{3... | collective-permute-start | bytes 933896 | tf_op jit(solution)/shard_map/ppermute | solution.py:61
  76.8 22.1 %collective-permute-start.3 = (bf16[64,2432]{1,0:T(8,128)(2,1)}, bf16[64,2432]{1,0:T(8,128)(2,1)}, u32[]{:S(2)}, u32[]{:S(2)}) collective-permute-start(bf16[64,2432]{1,0:T(8,128)(2,1)} %pad_maximum_fusion.14), channel_id=1, source_target_pairs={{0,256},{128,384},{256,0},{384,128},{1,257},{129,385},{257,1},{385... | collective-permute-start | bytes 933896 | tf_op jit(solution)/shard_map/ppermute | solution.py:61
  102.0 2.2 %copy-start.3 = (bf16[32,2,1152]{2,1,0:T(2,128)(2,1)S(1)}, bf16[32,2,1152]{2,1,0:T(2,128)(2,1)}, u32[]{:S(2)}) copy-start(bf16[32,2,1152]{2,1,0:T(2,128)(2,1)} %reshape.76) | copy-start | bytes 442372
  105.7 34.1 %all-to-all-start.1 = ((bf16[128,2,1152]{2,1,0:T(2,128)(2,1)}), bf16[128,2,1152]{2,1,0:T(2,128)(2,1)S(1)}, u32[]{:S(2)}, u32[]{:S(2)}) async-start(bf16[128,2,1152]{2,1,0:T(2,128)(2,1)} %constant_dynamic-update-slice_fusion), calls=%async_computation.1 | async-start | bytes 1179648 | tf_op jit(solution)/shard_map/all_to_all | solution.py:20
  124.7 15.4 %copy-start.5 = (bf16[24,128,2]{0,2,1:T(2,128)(2,1)S(1)}, bf16[24,128,2]{0,2,1:T(2,128)(2,1)}, u32[]{:S(2)}) copy-start(bf16[24,128,2]{0,2,1:T(2,128)(2,1)} %copy-done.4) | copy-start | bytes 36868

commit v3 on v1

--- a/solution.py
+++ b/solution.py
@@ -20,19 +20,17 @@
     return lax.all_to_all(x, axis, split_axis=0, concat_axis=0, tiled=True)
 
 
-def slot_tables(expert_ids, router_weight, experts, capacity):
-    rows = expert_ids.shape[0]
-    match = expert_ids[:, :, None] == jnp.arange(experts, dtype=jnp.int32)[None, None, :]
-    named = jnp.sum(match.astype(F32), axis=1)
-    weight = jnp.sum(jnp.where(match, router_weight.astype(F32)[:, :, None], 0.0), axis=1)
+def slot_tables(ids, weight, experts, capacity):
+    rows = ids.shape[1]
+    slot = jnp.arange(experts * capacity, dtype=jnp.int32)[:, None]
+    match = ids[:, None, :] == (slot // capacity)[None]
+    named = jnp.sum(match.astype(F32), axis=0)
+    share = jnp.sum(jnp.where(match, weight[:, None, :], 0.0), axis=0)
     row = jnp.arange(rows)
-    before = (row[None, :] < row[:, None]).astype(BF)
-    earlier = mm(before, named.astype(BF))
-    slot = jnp.arange(capacity, dtype=F32)
-    here = (earlier[:, :, None] == slot) & (named[:, :, None] > 0)
-    placing = here.astype(BF).reshape(rows, experts * capacity)
-    weighting = jnp.where(here, weight[:, :, None], 0.0).astype(BF)
-    return match, placing, weighting.reshape(rows, experts * capacity)
+    before = (row[:, None] < row[None, :]).astype(BF)
+    earlier = mm(named.astype(BF), before)
+    here = (named > 0) & (earlier == (slot % capacity).astype(F32))
+    return match, here, jnp.where(here, share, 0.0).astype(BF)
 
 
 def local(tokens, cotangent, router_weight, expert_ids, w_gate, w_up, w_down):
@@ -46,9 +44,11 @@
     part = total // reps
     gate_mat, up_mat, down_mat = w_gate[0], w_up[0], w_down[0]
 
-    match, placing, weighting = slot_tables(expert_ids, router_weight, experts, capacity)
+    weight = router_weight.T.astype(F32)
+    match, here, weighting = slot_tables(expert_ids.T, weight, experts, capacity)
+    placing = here.astype(BF)
     sent = jnp.concatenate(
-        [mm(placing, tokens, TN).astype(BF), mm(weighting, cotangent, TN).astype(BF)], axis=1
+        [mm(placing, tokens).astype(BF), mm(weighting, cotangent).astype(BF)], axis=1
     )
     recv = swap(sent.reshape(experts, capacity, 2 * width), "exp").reshape(total, 2 * width)
     inputs, out_delta = recv[:, :width], recv[:, width:]
@@ -86,12 +86,11 @@
     gate_grad = mm(inputs, gate_delta, TN).astype(BF)
     up_grad = mm(inputs, up_delta, TN).astype(BF)
 
-    mixed = mm(weighting, back[:, :width]).astype(BF)
-    token_grad = mm(placing, back[:, width : 2 * width]).astype(BF)
-    routed = back[:, 2 * width].astype(F32).reshape(1, experts, capacity)
-    by_expert = jnp.sum(placing.astype(F32).reshape(rows, experts, capacity) * routed, axis=2)
-    router_grad = jnp.sum(jnp.where(match, by_expert[:, None, :], 0.0), axis=2)
-    router_grad = (router_grad / router_weight.astype(F32)).astype(BF)
+    mixed = mm(weighting, back[:, :width], TN).astype(BF)
+    token_grad = mm(placing, back[:, width : 2 * width], TN).astype(BF)
+    routed = jnp.where(here, back[:, 2 * width :][:, :1].astype(F32), 0.0)
+    router_grad = jnp.sum(jnp.where(match, routed[None], 0.0), axis=1)
+    router_grad = (router_grad / weight).astype(BF).T
     return (mixed, token_grad, router_grad, gate_grad[None], up_grad[None], down_grad[None])
 
 

time: 121 us -> 120 us (level)
  local copies, waits for them, and re-layouts: 5.25 us -> 2.18 us
  other arithmetic: 1.45 us -> 3.03 us
    unnamed x11 -> x10, local copies, waits for them, and re-layouts: 2.61 us -> 0.35 us
    convert_element_type x3, other arithmetic: 0.12 us -> 1.35 us  [the longest x1 0.75 us: local(): weight = router_weight.T.astype(F32)]
where the time goes in v3:
time: 120 us; the launch traced here: 119 us
  blocking collectives  78.5 us (65%)
  waiting for transfers between devices  18.2 us (15%)
  matrix products  9.9 us (8%)
  starting transfers between devices  6.77 us (6%)
  other arithmetic  3.03 us (3%)
  local copies, waits for them, and re-layouts  2.18 us (2%)
    all_to_all x3, blocking collectives, swap(): return lax.all_to_all(x, axis, split_axis=0, concat_axis=0, tiled=True)  78.5 us
    all_to_all x1, waiting for transfers between devices, swap(): return lax.all_to_all(x, axis, split_axis=0, concat_axis=0, tiled=True)  18.2 us
    dot_general x14, matrix products, mm(): return lax.dot_general(a, b, dims, preferred_element_type=F32)  9.9 us
    all_to_all x1, starting transfers between devices, swap(): return lax.all_to_all(x, axis, split_axis=0, concat_axis=0, tiled=True)  6.77 us
  transfers between devices with their start and end apart: 1, of which 1 were waited for; matrix products, arithmetic and copies ran while one was open for 3% of the time, Pallas kernels for 0%

profile of v3, /device:TPU:1, one launch (start us, length us, event | category | flops | bytes accessed | tf_op | source)
XLA Modules:
  0.0 119.4 jit_solution(17480722781707377776)
XLA Ops:
  0.7 0.8 convert_bitcast_fusion
  1.4 0.8 fusion.23
  2.2 0.2 fusion.4
  2.4 1.0 convolution_convert_fusion.8
  3.4 1.0 convolution_convert_fusion.6
  4.5 0.2 reshape.93
  4.7 38.9 %all_to_all.20 = bf16[128,2,1024]{2,1,0:T(2,128)(2,1)S(1)} all-to-all(bf16[128,2,1024]{2,1,0:T(2,128)(2,1)S(1)} %reshape.93), channel_id=1, replica_groups=mesh['rep'=4,'exp'=128] {'exp'}, dimensions={0} | all-to-all | bytes 1048576 | tf_op jit(solution)/shard_map/all_to_all | solution.py:20
  43.7 0.2 reshape.94
  43.9 0.4 convolution_convert_fusion.4
  44.3 0.4 convolution_convert_fusion.3
  44.7 0.3 copy-done.1
  45.0 0.4 convolution_convert_fusion.5
  45.5 20.6 %all_to_all.21 = bf16[4,64,2304]{2,1,0:T(8,128)(2,1)S(1)} all-to-all(bf16[4,64,2304]{2,1,0:T(8,128)(2,1)S(1)} %bitcast.39), channel_id=1, replica_groups=mesh['rep'=4,'exp'=128] {'rep'}, dimensions={0} | all-to-all | bytes 2359296 | tf_op jit(solution)/shard_map/all_to_all | solution.py:20
  66.0 0.2 convert_reduce_fusion
  66.2 0.2 multiply_convert_fusion.1
  66.5 0.1 broadcast_in_dim.70
  66.6 19.0 %all_to_all.22 = bf16[4,64,2432]{2,1,0:T(8,128)(2,1)S(1)} all-to-all(bf16[4,64,2432]{2,1,0:T(8,128)(2,1)S(1)} %broadcast_in_dim.70), channel_id=1, replica_groups=mesh['rep'=4,'exp'=128] {'rep'}, dimensions={0} | all-to-all | bytes 2490368 | tf_op jit(solution)/shard_map/all_to_all | solution.py:20
  85.6 0.4 convolution_convert_fusion.7
  86.0 0.4 fusion.9
  86.4 0.4 fusion.3
  86.9 1.0 reshape.97
  87.9 6.8 %all-to-all-start.3 = ((bf16[128,2,1152]{2,1,0:T(2,128)(2,1)}), bf16[128,2,1152]{2,1,0:T(2,128)(2,1)S(1)}, u32[]{:S(2)}, u32[]{:S(2)}) async-start(bf16[128,2,1152]{2,1,0:T(2,128)(2,1)} %reshape.97), calls=%async_computation.3 | async-start | bytes 1179648 | tf_op jit(solution)/shard_map/all_to_all | solution.py:20
  94.7 1.3 %fusion = bf16[1,512,768]{2,1,0:T(8,128)(2,1)} fusion(bf16[256,2432]{1,0:T(8,128)(2,1)S(1)} %bitcast.36, bf16[256,1024]{1,0:T(8,128)(2,1)S(1)} %reshape.94), kind=kOutput, calls=%fused_computation.4 | convolution fusion | flops 201719808 | bytes 1441792 | tf_op jit(solution)/shard_map/dot_general | solution.py:12
  96.0 1.3 %fusion.1 = bf16[1,512,768]{2,1,0:T(8,128)(2,1)} fusion(bf16[256,2432]{1,0:T(8,128)(2,1)S(1)} %bitcast.37, bf16[256,1024]{1,0:T(8,128)(2,1)S(1)} %reshape.94), kind=kOutput, calls=%fused_computation.5 | convolution fusion | flops 201719808 | bytes 1441792 | tf_op jit(solution)/shard_map/dot_general | solution.py:12
  97.3 1.3 %fusion.2 = bf16[1,768,512]{2,1,0:T(8,128)(2,1)} fusion(bf16[256,2432]{1,0:T(8,128)(2,1)S(1)} %bitcast.38, bf16[256,1024]{1,0:T(8,128)(2,1)S(1)} %reshape.94), kind=kOutput, calls=%fused_computation.6 | convolution fusion | flops 201719808 | bytes 1441792 | tf_op jit(solution)/shard_map/dot_general | solution.py:12
  98.5 18.2 %all-to-all-done.3 = bf16[128,2,1152]{2,1,0:T(2,128)(2,1)S(1)} async-done(((bf16[128,2,1152]{2,1,0:T(2,128)(2,1)}), bf16[128,2,1152]{2,1,0:T(2,128)(2,1)S(1)}, u32[]{:S(2)}, u32[]{:S(2)}) %all-to-all-start.3) | async-done | bytes 589856 | tf_op jit(solution)/shard_map/all_to_all | solution.py:20
  116.7 0.2 reshape.98
  117.0 0.1 convert_reduce_fusion.1
  117.1 0.8 convolution_convert_fusion.10
  117.9 0.8 convolution_convert_fusion.9
  118.6 0.2 fusion.24
  118.8 0.6 fusion.31
  (18 shorter events, 0.3 us)
Async XLA Ops:
  0.6 43.6 %copy-start = (bf16[1,768,512]{2,1,0:T(8,128)(2,1)S(1)}, bf16[1,768,512]{2,1,0:T(8,128)(2,1)}, u32[]{:S(2)}) copy-start(bf16[1,768,512]{2,1,0:T(8,128)(2,1)} %param.13) | copy-start | bytes 2359300
  4.7 39.2 %copy-start.2 = (bf16[1,512,768]{2,1,0:T(8,128)(2,1)S(1)}, bf16[1,512,768]{2,1,0:T(8,128)(2,1)}, u32[]{:S(2)}) copy-start(bf16[1,512,768]{2,1,0:T(8,128)(2,1)} %param.12) | copy-start | bytes 2359300
  43.9 1.1 copy-start.1
  87.9 28.8 %all-to-all-start.3 = ((bf16[128,2,1152]{2,1,0:T(2,128)(2,1)}), bf16[128,2,1152]{2,1,0:T(2,128)(2,1)S(1)}, u32[]{:S(2)}, u32[]{:S(2)}) async-start(bf16[128,2,1152]{2,1,0:T(2,128)(2,1)} %reshape.97), calls=%async_computation.3 | async-start | bytes 1179648 | tf_op jit(solution)/shard_map/all_to_all | solution.py:20
  98.5 20.1 %copy-start.3 = (s32[24,8]{0,1:T(8,128)S(1)}, s32[24,8]{0,1:T(8,128)}, u32[]{:S(2)}) copy-start(s32[24,8]{0,1:T(8,128)} %param.10) | copy-start | bytes 2308
  98.5 20.3 %copy-start.4 = (bf16[24,8]{0,1:T(8,128)(2,1)S(1)}, bf16[24,8]{0,1:T(8,128)(2,1)}, u32[]{:S(2)}) copy-start(bf16[24,8]{0,1:T(8,128)(2,1)} %param.9) | copy-start | bytes 1156

commit v4 on v3

--- a/solution.py
+++ b/solution.py
@@ -1,6 +1,10 @@
+import functools
+
 import jax
 import jax.numpy as jnp
 from jax import lax
+from jax.experimental import pallas as pl
+from jax.experimental.pallas import tpu as pltpu
 from jax.sharding import PartitionSpec as P
 
 BF = jnp.bfloat16
@@ -20,17 +24,49 @@
     return lax.all_to_all(x, axis, split_axis=0, concat_axis=0, tiled=True)
 
 
-def slot_tables(ids, weight, experts, capacity):
-    rows = ids.shape[1]
-    slot = jnp.arange(experts * capacity, dtype=jnp.int32)[:, None]
-    match = ids[:, None, :] == (slot // capacity)[None]
-    named = jnp.sum(match.astype(F32), axis=0)
-    share = jnp.sum(jnp.where(match, weight[:, None, :], 0.0), axis=0)
-    row = jnp.arange(rows)
-    before = (row[:, None] < row[None, :]).astype(BF)
+def place_kernel(capacity, ids_ref, weight_ref, tokens_ref, cot_ref, sent_ref, placing_ref, weighting_ref):
+    top, rows = ids_ref.shape
+    experts = sent_ref.shape[0]
+    total = experts * capacity
+    width = sent_ref.shape[2] // 2
+    slot = lax.broadcasted_iota(jnp.int32, (total, rows), 0)
+    expert = slot // capacity
+    named = jnp.zeros((total, rows), F32)
+    share = jnp.zeros((total, rows), F32)
+    for k in range(top):
+        hit = ids_ref[k : k + 1, :] == expert
+        named = named + jnp.where(hit, 1.0, 0.0)
+        share = share + jnp.where(hit, weight_ref[k : k + 1, :].astype(F32), 0.0)
+    first = lax.broadcasted_iota(jnp.int32, (rows, rows), 0)
+    second = lax.broadcasted_iota(jnp.int32, (rows, rows), 1)
+    before = jnp.where(first < second, 1.0, 0.0).astype(BF)
     earlier = mm(named.astype(BF), before)
-    here = (named > 0) & (earlier == (slot % capacity).astype(F32))
-    return match, here, jnp.where(here, share, 0.0).astype(BF)
+    here = (named > 0.0) & (earlier == (slot % capacity).astype(F32))
+    placing = jnp.where(here, 1.0, 0.0).astype(BF)
+    weighting = jnp.where(here, share, 0.0).astype(BF)
+    placing_ref[...] = placing
+    weighting_ref[...] = weighting
+    shape = (experts, capacity, width)
+    sent_ref[:, :, :width] = mm(placing, tokens_ref[...]).astype(BF).reshape(shape)
+    sent_ref[:, :, width:] = mm(weighting, cot_ref[...]).astype(BF).reshape(shape)
+
+
+def combine_kernel(
+    capacity, ids_ref, weight_ref, placing_ref, weighting_ref, back_ref, mixed_ref, grad_ref, router_ref
+):
+    top, rows = ids_ref.shape
+    total = placing_ref.shape[0]
+    width = mixed_ref.shape[1]
+    mixed_ref[...] = mm(weighting_ref[...], back_ref[:, :width], TN).astype(BF)
+    grad_ref[...] = mm(placing_ref[...], back_ref[:, width : 2 * width], TN).astype(BF)
+    expert = lax.broadcasted_iota(jnp.int32, (total, rows), 0) // capacity
+    routed = back_ref[:, 2 * width :].astype(F32)[:, :rows] * placing_ref[...].astype(F32)
+    sums = [
+        jnp.sum(jnp.where(ids_ref[k : k + 1, :] == expert, routed, 0.0), axis=0, keepdims=True)
+        for k in range(top)
+    ]
+    sums = jnp.concatenate(sums, axis=0) / weight_ref[...].astype(F32)
+    router_ref[...] = sums.astype(BF)
 
 
 def local(tokens, cotangent, router_weight, expert_ids, w_gate, w_up, w_down):
@@ -44,13 +80,20 @@
     part = total // reps
     gate_mat, up_mat, down_mat = w_gate[0], w_up[0], w_down[0]
 
-    weight = router_weight.T.astype(F32)
-    match, here, weighting = slot_tables(expert_ids.T, weight, experts, capacity)
-    placing = here.astype(BF)
-    sent = jnp.concatenate(
-        [mm(placing, tokens).astype(BF), mm(weighting, cotangent).astype(BF)], axis=1
-    )
-    recv = swap(sent.reshape(experts, capacity, 2 * width), "exp").reshape(total, 2 * width)
+    ids, weight = expert_ids.T, router_weight.T
+    sent, placing, weighting = pl.pallas_call(
+        functools.partial(place_kernel, capacity),
+        out_shape=(
+            jax.ShapeDtypeStruct((experts, capacity, 2 * width), BF),
+            jax.ShapeDtypeStruct((total, rows), BF),
+            jax.ShapeDtypeStruct((total, rows), BF),
+        ),
+        name="place",
+        in_specs=[pl.BlockSpec(memory_space=pltpu.VMEM)] * 4,
+        out_specs=(pl.BlockSpec(memory_space=pltpu.VMEM),) * 3,
+        compiler_params=pltpu.CompilerParams(vmem_limit_bytes=6 * 1024 * 1024),
+    )(ids, weight, tokens, cotangent)
+    recv = swap(sent, "exp").reshape(total, 2 * width)
     inputs, out_delta = recv[:, :width], recv[:, width:]
 
     partial = jnp.concatenate(
@@ -86,11 +129,19 @@
     gate_grad = mm(inputs, gate_delta, TN).astype(BF)
     up_grad = mm(inputs, up_delta, TN).astype(BF)
 
-    mixed = mm(weighting, back[:, :width], TN).astype(BF)
-    token_grad = mm(placing, back[:, width : 2 * width], TN).astype(BF)
-    routed = jnp.where(here, back[:, 2 * width :][:, :1].astype(F32), 0.0)
-    router_grad = jnp.sum(jnp.where(match, routed[None], 0.0), axis=1)
-    router_grad = (router_grad / weight).astype(BF).T
+    mixed, token_grad, router_grad = pl.pallas_call(
+        functools.partial(combine_kernel, capacity),
+        out_shape=(
+            jax.ShapeDtypeStruct((rows, width), BF),
+            jax.ShapeDtypeStruct((rows, width), BF),
+            jax.ShapeDtypeStruct((top, rows), BF),
+        ),
+        name="combine",
+        in_specs=[pl.BlockSpec(memory_space=pltpu.VMEM)] * 5,
+        out_specs=(pl.BlockSpec(memory_space=pltpu.VMEM),) * 3,
+        compiler_params=pltpu.CompilerParams(vmem_limit_bytes=6 * 1024 * 1024),
+    )(ids, weight, placing, weighting, back)
+    router_grad = router_grad.T
     return (mixed, token_grad, router_grad, gate_grad[None], up_grad[None], down_grad[None])
 
 

time: 120 us -> 117 us (0.975)
  matrix products: 9.9 us -> 6.16 us
  local copies, waits for them, and re-layouts: 2.18 us -> 4.88 us
  other arithmetic: 3.03 us -> 0.54 us
  Pallas kernels: 0 us -> 1.34 us
    dot_general x14 -> x9, matrix products: 9.9 us -> 6.16 us  [mm(): return lax.dot_general(a, b, dims, preferred_element_type=F32)]
    unnamed x10 -> x18, local copies, waits for them, and re-layouts: 0.35 us -> 3.26 us
    convert_element_type x3 -> x0, other arithmetic: 1.35 us -> none  [the longest x1 0.75 us: local(): weight = router_weight.T.astype(F32)]
    pallas_call x0 -> x2, Pallas kernels: none -> 1.34 us  [the longest x1 0.88 us: local(): pl.pallas_call(functools.partial(combine_kernel, capacity), out_shape=(ja...]
where the time goes in v4:
time: 117 us
  blocking collectives  78.3 us (67%)
  waiting for transfers between devices  18.2 us (16%)
  starting transfers between devices  6.77 us (6%)
  matrix products  6.16 us (5%)
  local copies, waits for them, and re-layouts  4.88 us (4%)
  Pallas kernels  1.34 us (1%)
    all_to_all x3, blocking collectives, swap(): return lax.all_to_all(x, axis, split_axis=0, concat_axis=0, tiled=True)  78.3 us
    all_to_all x1, waiting for transfers between devices, swap(): return lax.all_to_all(x, axis, split_axis=0, concat_axis=0, tiled=True)  18.2 us
    all_to_all x1, starting transfers between devices, swap(): return lax.all_to_all(x, axis, split_axis=0, concat_axis=0, tiled=True)  6.77 us
    dot_general x9, matrix products, mm(): return lax.dot_general(a, b, dims, preferred_element_type=F32)  6.16 us
    unnamed x18, local copies, waits for them, and re-layouts  3.26 us
  transfers between devices with their start and end apart: 1, of which 1 were waited for; matrix products, arithmetic and copies ran while one was open for 3% of the time, Pallas kernels for 0%

profile of v4, /device:TPU:1, one launch (start us, length us, event | category | flops | bytes accessed | tf_op | source)
XLA Modules:
  0.0 117.1 jit_solution(17473989223159720039)
XLA Ops:
  0.6 0.0 copy-start
  0.6 0.0 copy-start.1
  0.7 0.8 copy-done.1
  1.5 0.7 copy-done.2
  2.2 0.7 copy-done.3
  2.9 0.7 copy-done.5
  3.6 0.5 place.1
  4.0 38.8 %all_to_all.20 = bf16[128,2,1024]{2,1,0:T(2,128)(2,1)S(1)} all-to-all(bf16[128,2,1024]{2,1,0:T(2,128)(2,1)S(1)} %get-tuple-element.14), channel_id=1, replica_groups=mesh['rep'=4,'exp'=128] {'exp'}, dimensions={0} | all-to-all | bytes 1048576 | tf_op jit(solution)/shard_map/all_to_all | solution.py:24
  42.8 0.2 reshape.32
  43.1 0.0 copy-start.7
  43.1 0.4 convolution_convert_fusion.4
  43.5 0.4 convolution_convert_fusion.3
  43.9 0.3 copy-done.7
  44.2 0.4 convolution_convert_fusion.5
  44.6 0.1 pad_maximum_fusion
  44.7 20.6 %all_to_all.21 = bf16[4,64,2304]{2,1,0:T(8,128)(2,1)S(1)} all-to-all(bf16[4,64,2304]{2,1,0:T(8,128)(2,1)S(1)} %bitcast.37), channel_id=1, replica_groups=mesh['rep'=4,'exp'=128] {'rep'}, dimensions={0} | all-to-all | bytes 2359296 | tf_op jit(solution)/shard_map/all_to_all | solution.py:24
  65.2 0.2 convert_reduce_fusion
  65.4 0.2 multiply_convert_fusion.1
  65.6 0.1 broadcast_in_dim.10
  65.7 0.1 broadcast_in_dim.22
  65.8 19.0 %all_to_all.22 = bf16[4,64,2432]{2,1,0:T(8,128)(2,1)S(1)} all-to-all(bf16[4,64,2432]{2,1,0:T(8,128)(2,1)S(1)} %broadcast_in_dim.22), channel_id=1, replica_groups=mesh['rep'=4,'exp'=128] {'rep'}, dimensions={0} | all-to-all | bytes 2490368 | tf_op jit(solution)/shard_map/all_to_all | solution.py:24
  84.8 0.4 convolution_convert_fusion.6
  85.2 0.4 fusion.8
  85.6 0.4 fusion.3
  86.0 1.0 reshape.35
  87.1 6.8 %all-to-all-start.3 = ((bf16[128,2,1152]{2,1,0:T(2,128)(2,1)}), bf16[128,2,1152]{2,1,0:T(2,128)(2,1)S(1)}, u32[]{:S(2)}, u32[]{:S(2)}) async-start(bf16[128,2,1152]{2,1,0:T(2,128)(2,1)} %reshape.35), calls=%async_computation.3 | async-start | bytes 1179648 | tf_op jit(solution)/shard_map/all_to_all | solution.py:24
  93.9 1.3 %fusion = bf16[1,512,768]{2,1,0:T(8,128)(2,1)} fusion(bf16[256,2432]{1,0:T(8,128)(2,1)S(1)} %bitcast.34, bf16[256,1024]{1,0:T(8,128)(2,1)S(1)} %reshape.32), kind=kOutput, calls=%fused_computation.4 | convolution fusion | flops 201719808 | bytes 1441792 | tf_op jit(solution)/shard_map/dot_general | solution.py:16
  95.2 1.3 %fusion.1 = bf16[1,512,768]{2,1,0:T(8,128)(2,1)} fusion(bf16[256,2432]{1,0:T(8,128)(2,1)S(1)} %bitcast.35, bf16[256,1024]{1,0:T(8,128)(2,1)S(1)} %reshape.32), kind=kOutput, calls=%fused_computation.5 | convolution fusion | flops 201719808 | bytes 1441792 | tf_op jit(solution)/shard_map/dot_general | solution.py:16
  96.5 1.3 %fusion.2 = bf16[1,768,512]{2,1,0:T(8,128)(2,1)} fusion(bf16[256,2432]{1,0:T(8,128)(2,1)S(1)} %bitcast.36, bf16[256,1024]{1,0:T(8,128)(2,1)S(1)} %reshape.32), kind=kOutput, calls=%fused_computation.6 | convolution fusion | flops 201719808 | bytes 1441792 | tf_op jit(solution)/shard_map/dot_general | solution.py:16
  97.7 18.2 %all-to-all-done.3 = bf16[128,2,1152]{2,1,0:T(2,128)(2,1)S(1)} async-done(((bf16[128,2,1152]{2,1,0:T(2,128)(2,1)}), bf16[128,2,1152]{2,1,0:T(2,128)(2,1)S(1)}, u32[]{:S(2)}, u32[]{:S(2)}) %all-to-all-start.3) | async-done | bytes 589856 | tf_op jit(solution)/shard_map/all_to_all | solution.py:24
  115.9 0.2 reshape.36.back_ref
  116.2 0.9 combine.1
  (13 shorter events, 0.1 us)
Async XLA Ops:
  0.6 42.8 %copy-start = (bf16[1,768,512]{2,1,0:T(8,128)(2,1)S(1)}, bf16[1,768,512]{2,1,0:T(8,128)(2,1)}, u32[]{:S(2)}) copy-start(bf16[1,768,512]{2,1,0:T(8,128)(2,1)} %param.13) | copy-start | bytes 2359300
  0.6 0.8 copy-start.1
  1.5 0.7 copy-start.2
  2.2 0.7 copy-start.3
  2.9 0.7 copy-start.5
  3.6 39.5 %copy-start.8 = (bf16[1,512,768]{2,1,0:T(8,128)(2,1)S(1)}, bf16[1,512,768]{2,1,0:T(8,128)(2,1)}, u32[]{:S(2)}) copy-start(bf16[1,512,768]{2,1,0:T(8,128)(2,1)} %param.12) | copy-start | bytes 2359300
  43.1 1.1 copy-start.7
  87.1 28.8 %all-to-all-start.3 = ((bf16[128,2,1152]{2,1,0:T(2,128)(2,1)}), bf16[128,2,1152]{2,1,0:T(2,128)(2,1)S(1)}, u32[]{:S(2)}, u32[]{:S(2)}) async-start(bf16[128,2,1152]{2,1,0:T(2,128)(2,1)} %reshape.35), calls=%async_computation.3 | async-start | bytes 1179648 | tf_op jit(solution)/shard_map/all_to_all | solution.py:24
  96.4 19.7 %copy-start.4 = (s32[24,8]{0,1:T(8,128)S(1)}, s32[24,8]{0,1:T(8,128)}, u32[]{:S(2)}) copy-start(s32[24,8]{0,1:T(8,128)} %param.10) | copy-start | bytes 2308
  96.5 19.7 %copy-start.6 = (bf16[24,8]{0,1:T(8,128)(2,1)S(1)}, bf16[24,8]{0,1:T(8,128)(2,1)}, u32[]{:S(2)}) copy-start(bf16[24,8]{0,1:T(8,128)(2,1)} %param.9) | copy-start | bytes 1156

commit v5 on v4

--- a/solution.py
+++ b/solution.py
@@ -24,7 +24,31 @@
     return lax.all_to_all(x, axis, split_axis=0, concat_axis=0, tiled=True)
 
 
-def place_kernel(capacity, ids_ref, weight_ref, tokens_ref, cot_ref, sent_ref, placing_ref, weighting_ref):
+def place_kernel(
+    capacity,
+    ids_hbm,
+    weight_hbm,
+    tokens_hbm,
+    cot_hbm,
+    sent_ref,
+    placing_ref,
+    weighting_ref,
+    ids_ref,
+    weight_ref,
+    tokens_ref,
+    cot_ref,
+    arrived,
+):
+    sources = (ids_hbm, weight_hbm, tokens_hbm, cot_hbm)
+    buffers = (ids_ref, weight_ref, tokens_ref, cot_ref)
+    copies = [
+        pltpu.make_async_copy(source, buffer, arrived.at[i])
+        for i, (source, buffer) in enumerate(zip(sources, buffers))
+    ]
+    for copy in copies:
+        copy.start()
+    copies[0].wait()
+    copies[1].wait()
     top, rows = ids_ref.shape
     experts = sent_ref.shape[0]
     total = experts * capacity
@@ -47,8 +71,56 @@
     placing_ref[...] = placing
     weighting_ref[...] = weighting
     shape = (experts, capacity, width)
+    copies[2].wait()
     sent_ref[:, :, :width] = mm(placing, tokens_ref[...]).astype(BF).reshape(shape)
+    copies[3].wait()
     sent_ref[:, :, width:] = mm(weighting, cot_ref[...]).astype(BF).reshape(shape)
+
+
+def activate_kernel(pieces_ref, mine_ref):
+    reps, part, triple = pieces_ref.shape
+    hid = triple // 3
+
+    def summed(i):
+        terms = [pieces_ref[r, :, i * hid : (i + 1) * hid].astype(F32) for r in range(reps)]
+        return functools.reduce(lambda a, b: a + b, terms)
+
+    gate, upval, hidden_delta = summed(0), summed(1), summed(2)
+    sigmoid = 1.0 / (1.0 + jnp.exp(-gate))
+    active = gate * sigmoid
+    hidden = (active * upval).astype(BF)
+    gate_delta = (hidden_delta * upval * sigmoid * (1.0 + gate * (1.0 - sigmoid))).astype(BF)
+    up_delta = (hidden_delta * active).astype(BF)
+    scaled = jnp.sum(hidden.astype(F32) * hidden_delta, axis=1, keepdims=True)
+    scaled = jnp.broadcast_to(scaled, (part, LANES)).astype(BF)
+    for r in range(reps):
+        mine_ref[r, :, :hid] = hidden
+        mine_ref[r, :, hid : 2 * hid] = gate_delta
+        mine_ref[r, :, 2 * hid : 3 * hid] = up_delta
+        mine_ref[r, :, 3 * hid :] = scaled
+
+
+def expand_kernel(full_ref, gate_ref, up_ref, down_ref, back_hbm, back_ref, leaving):
+    hid, width = down_ref.shape
+    capacity = back_ref.shape[1]
+    chunks = leaving.shape[0]
+    rows = full_ref.shape[0] // chunks
+    copies = []
+    for i in range(chunks):
+        full = full_ref[i * rows : (i + 1) * rows, :]
+        outputs = mm(full[:, :hid], down_ref[...]).astype(BF)
+        token_delta = mm(full[:, hid : 2 * hid], gate_ref[...], NT)
+        token_delta = (token_delta + mm(full[:, 2 * hid : 3 * hid], up_ref[...], NT)).astype(BF)
+        mine = pl.ds(i * rows // capacity, rows // capacity)
+        shape = (rows // capacity, capacity, width)
+        back_ref[mine, :, :width] = outputs.reshape(shape)
+        back_ref[mine, :, width : 2 * width] = token_delta.reshape(shape)
+        back_ref[mine, :, 2 * width :] = full[:, 3 * hid :].reshape(shape[:2] + (LANES,))
+        copy = pltpu.make_async_copy(back_ref.at[mine], back_hbm.at[mine], leaving.at[i])
+        copy.start()
+        copies.append(copy)
+    for copy in copies:
+        copy.wait()
 
 
 def combine_kernel(
@@ -57,10 +129,11 @@
     top, rows = ids_ref.shape
     total = placing_ref.shape[0]
     width = mixed_ref.shape[1]
-    mixed_ref[...] = mm(weighting_ref[...], back_ref[:, :width], TN).astype(BF)
-    grad_ref[...] = mm(placing_ref[...], back_ref[:, width : 2 * width], TN).astype(BF)
+    back = back_ref[...].reshape(total, back_ref.shape[2])
+    mixed_ref[...] = mm(weighting_ref[...], back[:, :width], TN).astype(BF)
+    grad_ref[...] = mm(placing_ref[...], back[:, width : 2 * width], TN).astype(BF)
     expert = lax.broadcasted_iota(jnp.int32, (total, rows), 0) // capacity
-    routed = back_ref[:, 2 * width :].astype(F32)[:, :rows] * placing_ref[...].astype(F32)
+    routed = back[:, 2 * width :].astype(F32)[:, :rows] * placing_ref[...].astype(F32)
     sums = [
         jnp.sum(jnp.where(ids_ref[k : k + 1, :] == expert, routed, 0.0), axis=0, keepdims=True)
         for k in range(top)
@@ -89,10 +162,17 @@
             jax.ShapeDtypeStruct((total, rows), BF),
         ),
         name="place",
-        in_specs=[pl.BlockSpec(memory_space=pltpu.VMEM)] * 4,
+        in_specs=[pl.BlockSpec(memory_space=pltpu.HBM)] * 4,
         out_specs=(pl.BlockSpec(memory_space=pltpu.VMEM),) * 3,
+        scratch_shapes=[
+            pltpu.VMEM((top, rows), jnp.int32),
+            pltpu.VMEM((top, rows), BF),
+            pltpu.VMEM((rows, width), BF),
+            pltpu.VMEM((rows, width), BF),
+            pltpu.SemaphoreType.DMA((4,)),
+        ],
         compiler_params=pltpu.CompilerParams(vmem_limit_bytes=6 * 1024 * 1024),
-    )(ids, weight, tokens, cotangent)
+    )(*(pltpu.with_memory_space_constraint(a, pltpu.HBM) for a in (ids, weight, tokens, cotangent)))
     recv = swap(sent, "exp").reshape(total, 2 * width)
     inputs, out_delta = recv[:, :width], recv[:, width:]
 
@@ -105,25 +185,29 @@
         axis=1,
     )
     pieces = swap(partial.reshape(reps, part, 3 * hid), "rep")
-    summed = jnp.sum(pieces.astype(F32), axis=0)
-    gate, upval, hidden_delta = summed[:, :hid], summed[:, hid : 2 * hid], summed[:, 2 * hid :]
-    sigmoid = 1.0 / (1.0 + jnp.exp(-gate))
-    active = gate * sigmoid
-    hidden = (active * upval).astype(BF)
-    gate_delta = (hidden_delta * upval * sigmoid * (1.0 + gate * (1.0 - sigmoid))).astype(BF)
-    up_delta = (hidden_delta * active).astype(BF)
-    scaled = jnp.sum(hidden.astype(F32) * hidden_delta, axis=1, keepdims=True).astype(BF)
-    mine = jnp.concatenate(
-        [hidden, gate_delta, up_delta, jnp.broadcast_to(scaled, (part, LANES))], axis=1
-    )
-    full = swap(jnp.broadcast_to(mine[None], (reps,) + mine.shape), "rep").reshape(total, -1)
+    mine = pl.pallas_call(
+        activate_kernel,
+        out_shape=jax.ShapeDtypeStruct((reps, part, 3 * hid + LANES), BF),
+        name="activate",
+        in_specs=[pl.BlockSpec(memory_space=pltpu.VMEM)],
+        out_specs=pl.BlockSpec(memory_space=pltpu.VMEM),
+        compiler_params=pltpu.CompilerParams(vmem_limit_bytes=8 * 1024 * 1024),
+    )(pieces)
+    full = swap(mine, "rep").reshape(total, -1)
     hidden, gate_delta = full[:, :hid], full[:, hid : 2 * hid]
-    up_delta, scaled = full[:, 2 * hid : 3 * hid], full[:, 3 * hid :]
-
-    outputs = mm(hidden, down_mat).astype(BF)
-    token_delta = (mm(gate_delta, gate_mat, NT) + mm(up_delta, up_mat, NT)).astype(BF)
-    back = jnp.concatenate([outputs, token_delta, scaled], axis=1)
-    back = swap(back.reshape(experts, capacity, back.shape[1]), "exp").reshape(total, -1)
+    up_delta = full[:, 2 * hid : 3 * hid]
+
+    shape = (experts, capacity, 2 * width + LANES)
+    back = pl.pallas_call(
+        expand_kernel,
+        out_shape=jax.ShapeDtypeStruct(shape, BF),
+        name="expand",
+        in_specs=[pl.BlockSpec(memory_space=pltpu.VMEM)] * 4,
+        out_specs=pl.BlockSpec(memory_space=pltpu.HBM),
+        scratch_shapes=[pltpu.VMEM(shape, BF), pltpu.SemaphoreType.DMA((2,))],
+        compiler_params=pltpu.CompilerParams(vmem_limit_bytes=12 * 1024 * 1024),
+    )(full, gate_mat, up_mat, down_mat)
+    back = swap(back, "exp")
 
     down_grad = mm(hidden, out_delta, TN).astype(BF)
     gate_grad = mm(inputs, gate_delta, TN).astype(BF)

time: 117 us -> 115 us (0.983)
  local copies, waits for them, and re-layouts: 4.88 us -> 0.75 us
  Pallas kernels: 1.34 us -> 5.02 us
  matrix products: 6.16 us -> 4.99 us
    unnamed x18 -> x10, local copies, waits for them, and re-layouts: 3.26 us -> 0.55 us
    pallas_call x0 -> x2, Pallas kernels: none -> 2.5 us  [the longest x1 2.14 us: local(): pl.pallas_call(expand_kernel, out_shape=jax.ShapeDtypeStruct(shape, BF),...]
    reshape x2 -> x0, local copies, waits for them, and re-layouts: 1.26 us -> none  [the longest x1 1.04 us: local(): back.reshape(experts, capacity, back.shape[1])]
    dot_general x9 -> x6, matrix products: 6.16 us -> 4.99 us  [mm(): return lax.dot_general(a, b, dims, preferred_element_type=F32)]
where the time goes in v5:
time: 115 us
  blocking collectives  78.3 us (68%)
  waiting for transfers between devices  18.2 us (16%)
  starting transfers between devices  6.79 us (6%)
  Pallas kernels  5.02 us (4%)
  matrix products  4.99 us (4%)
    all_to_all x3, blocking collectives, swap(): return lax.all_to_all(x, axis, split_axis=0, concat_axis=0, tiled=True)  78.3 us
    all_to_all x1, waiting for transfers between devices, swap(): return lax.all_to_all(x, axis, split_axis=0, concat_axis=0, tiled=True)  18.2 us
    all_to_all x1, starting transfers between devices, swap(): return lax.all_to_all(x, axis, split_axis=0, concat_axis=0, tiled=True)  6.79 us
    dot_general x6, matrix products, mm(): return lax.dot_general(a, b, dims, preferred_element_type=F32)  4.99 us
  transfers between devices with their start and end apart: 1, of which 1 were waited for; matrix products, arithmetic and copies ran while one was open for 3% of the time, Pallas kernels for 0%

profile of v5, /device:TPU:1, one launch (start us, length us, event | category | flops | bytes accessed | tf_op | source)
XLA Modules:
  0.0 114.9 jit_solution(11525223495596053107)
XLA Ops:
  0.6 0.0 copy-start.1
  0.6 1.6 %place.1 = (bf16[128,2,1024]{2,1,0:T(2,128)(2,1)S(1)}, bf16[256,24]{1,0:T(8,128)(2,1)S(1)}, bf16[256,24]{1,0:T(8,128)(2,1)S(1)}) custom-call(s32[8,24]{1,0:T(8,128)} %bitcast.27, bf16[8,24]{1,0:T(8,128)(2,1)} %bitcast.29, bf16[24,512]{1,0:T(8,128)(2,1)} %tokens_hbm.1, bf16[24,512]{1,0:T(8,128)(2,1)} %cot_hbm.1), custom_call_target="tpu_custom_call" | custom-call | tf_op jit(solution)/shard_map/place/pallas_call | solution.py:157
  2.2 38.8 %all_to_all.20 = bf16[128,2,1024]{2,1,0:T(2,128)(2,1)S(1)} all-to-all(bf16[128,2,1024]{2,1,0:T(2,128)(2,1)S(1)} %get-tuple-element.14), channel_id=1, replica_groups=mesh['rep'=4,'exp'=128] {'exp'}, dimensions={0} | all-to-all | bytes 1048576 | tf_op jit(solution)/shard_map/all_to_all | solution.py:24
  41.0 0.0 copy-start
  41.0 0.2 reshape.21
  41.2 0.0 copy-done.1
  41.2 0.0 copy-start.2
  41.2 0.4 convolution_convert_fusion.4
  41.6 0.5 copy-done
  42.1 0.4 convolution_convert_fusion.3
  42.5 0.0 copy-done.2
  42.5 0.4 convolution_convert_fusion.5
  42.9 0.1 pad_maximum_fusion
  43.0 20.6 %all_to_all.21.pieces_ref = bf16[4,64,2304]{2,1,0:T(8,128)(2,1)S(1)} all-to-all(bf16[4,64,2304]{2,1,0:T(8,128)(2,1)S(1)} %bitcast.31), channel_id=1, replica_groups=mesh['rep'=4,'exp'=128] {'rep'}, dimensions={0} | all-to-all | bytes 2359296 | tf_op jit(solution)/shard_map/all_to_all | solution.py:24
  63.6 0.4 activate.1
  64.0 19.0 %all_to_all.22 = bf16[4,64,2432]{2,1,0:T(8,128)(2,1)S(1)} all-to-all(bf16[4,64,2432]{2,1,0:T(8,128)(2,1)S(1)} %activate.1), channel_id=1, replica_groups=mesh['rep'=4,'exp'=128] {'rep'}, dimensions={0} | all-to-all | bytes 2490368 | tf_op jit(solution)/shard_map/all_to_all | solution.py:24
  82.9 2.1 %expand.1 = bf16[128,2,1152]{2,1,0:T(2,128)(2,1)} custom-call(bf16[256,2432]{1,0:T(8,128)(2,1)S(1)} %bitcast.20, bf16[512,768]{1,0:T(8,128)(2,1)S(1)} %bitcast.26, bf16[512,768]{1,0:T(8,128)(2,1)S(1)} %bitcast.25, bf16[768,512]{1,0:T(8,128)(2,1)S(1)} %bitcast.24), custom_call_target="tpu_custom_call" | custom-call | tf_op jit(solution)/shard_map/expand/pallas_call | solution.py:201
  85.1 6.8 %all-to-all-start.3 = ((bf16[128,2,1152]{2,1,0:T(2,128)(2,1)}), bf16[128,2,1152]{2,1,0:T(2,128)(2,1)S(1)}, u32[]{:S(2)}, u32[]{:S(2)}) async-start(bf16[128,2,1152]{2,1,0:T(2,128)(2,1)} %expand.1), calls=%async_computation.3 | async-start | bytes 1179648 | tf_op jit(solution)/shard_map/all_to_all | solution.py:24
  91.9 1.3 %fusion.1 = bf16[1,512,768]{2,1,0:T(8,128)(2,1)} fusion(bf16[256,2432]{1,0:T(8,128)(2,1)S(1)} %bitcast.21, bf16[256,1024]{1,0:T(8,128)(2,1)S(1)} %reshape.21), kind=kOutput, calls=%fused_computation.4 | convolution fusion | flops 201719808 | bytes 1441792 | tf_op jit(solution)/shard_map/dot_general | solution.py:16
  93.2 0.0 copy-start.3
  93.2 0.0 copy-start.4
  93.2 1.3 %fusion = bf16[1,512,768]{2,1,0:T(8,128)(2,1)} fusion(bf16[256,2432]{1,0:T(8,128)(2,1)S(1)} %bitcast.22, bf16[256,1024]{1,0:T(8,128)(2,1)S(1)} %reshape.21), kind=kOutput, calls=%fused_computation.3 | convolution fusion | flops 201719808 | bytes 1441792 | tf_op jit(solution)/shard_map/dot_general | solution.py:16
  94.5 1.3 %fusion.2 = bf16[1,768,512]{2,1,0:T(8,128)(2,1)} fusion(bf16[256,2432]{1,0:T(8,128)(2,1)S(1)} %bitcast.23, bf16[256,1024]{1,0:T(8,128)(2,1)S(1)} %reshape.21), kind=kOutput, calls=%fused_computation.5 | convolution fusion | flops 201719808 | bytes 1441792 | tf_op jit(solution)/shard_map/dot_general | solution.py:16
  95.7 18.2 %all-to-all-done.3.back_ref = bf16[128,2,1152]{2,1,0:T(2,128)(2,1)S(1)} async-done(((bf16[128,2,1152]{2,1,0:T(2,128)(2,1)}), bf16[128,2,1152]{2,1,0:T(2,128)(2,1)S(1)}, u32[]{:S(2)}, u32[]{:S(2)}) %all-to-all-start.3) | async-done | bytes 589856 | tf_op jit(solution)/shard_map/all_to_all | solution.py:24
  113.9 0.0 copy-done.3
  114.0 0.0 copy-done.4
  114.0 1.0 combine.1
Async XLA Ops:
  0.6 40.6 %copy-start.1 = (bf16[1,512,768]{2,1,0:T(8,128)(2,1)S(1)}, bf16[1,512,768]{2,1,0:T(8,128)(2,1)}, u32[]{:S(2)}) copy-start(bf16[1,512,768]{2,1,0:T(8,128)(2,1)} %param.12) | copy-start | bytes 2359300
  41.0 1.1 copy-start
  41.2 1.3 %copy-start.2 = (bf16[1,512,768]{2,1,0:T(8,128)(2,1)S(1)}, bf16[1,512,768]{2,1,0:T(8,128)(2,1)}, u32[]{:S(2)}) copy-start(bf16[1,512,768]{2,1,0:T(8,128)(2,1)} %param.11) | copy-start | bytes 2359300
  85.1 28.9 %all-to-all-start.3 = ((bf16[128,2,1152]{2,1,0:T(2,128)(2,1)}), bf16[128,2,1152]{2,1,0:T(2,128)(2,1)S(1)}, u32[]{:S(2)}, u32[]{:S(2)}) async-start(bf16[128,2,1152]{2,1,0:T(2,128)(2,1)} %expand.1), calls=%async_computation.3 | async-start | bytes 1179648 | tf_op jit(solution)/shard_map/all_to_all | solution.py:24
  93.2 20.8 %copy-start.3 = (s32[24,8]{0,1:T(8,128)S(1)}, s32[24,8]{0,1:T(8,128)}, u32[]{:S(2)}) copy-start(s32[24,8]{0,1:T(8,128)} %param.10) | copy-start | bytes 2308
  93.2 20.8 %copy-start.4 = (bf16[24,8]{0,1:T(8,128)(2,1)S(1)}, bf16[24,8]{0,1:T(8,128)(2,1)}, u32[]{:S(2)}) copy-start(bf16[24,8]{0,1:T(8,128)(2,1)} %param.9) | copy-start | bytes 1156

commit v6 on v5

--- a/solution.py
+++ b/solution.py
@@ -30,17 +30,23 @@
     weight_hbm,
     tokens_hbm,
     cot_hbm,
+    gate_hbm,
+    up_hbm,
+    down_hbm,
     sent_ref,
     placing_ref,
     weighting_ref,
+    gate_ref,
+    up_ref,
+    down_ref,
     ids_ref,
     weight_ref,
     tokens_ref,
     cot_ref,
     arrived,
 ):
-    sources = (ids_hbm, weight_hbm, tokens_hbm, cot_hbm)
-    buffers = (ids_ref, weight_ref, tokens_ref, cot_ref)
+    sources = (ids_hbm, weight_hbm, tokens_hbm, cot_hbm, gate_hbm, up_hbm, down_hbm)
+    buffers = (ids_ref, weight_ref, tokens_ref, cot_ref, gate_ref, up_ref, down_ref)
     copies = [
         pltpu.make_async_copy(source, buffer, arrived.at[i])
         for i, (source, buffer) in enumerate(zip(sources, buffers))
@@ -75,6 +81,19 @@
     sent_ref[:, :, :width] = mm(placing, tokens_ref[...]).astype(BF).reshape(shape)
     copies[3].wait()
     sent_ref[:, :, width:] = mm(weighting, cot_ref[...]).astype(BF).reshape(shape)
+    for copy in copies[4:]:
+        copy.wait()
+
+
+def partial_kernel(recv_ref, gate_ref, up_ref, down_ref, out_ref):
+    experts, capacity, both = recv_ref.shape
+    hid = gate_ref.shape[1]
+    shape = (experts * capacity, both // 2)
+    inputs = recv_ref[:, :, : both // 2].reshape(shape)
+    out_delta = recv_ref[:, :, both // 2 :].reshape(shape)
+    out_ref[:, :hid] = mm(inputs, gate_ref[...]).astype(BF)
+    out_ref[:, hid : 2 * hid] = mm(inputs, up_ref[...]).astype(BF)
+    out_ref[:, 2 * hid :] = mm(out_delta, down_ref[...], NT).astype(BF)
 
 
 def activate_kernel(pieces_ref, mine_ref):
@@ -102,25 +121,26 @@
 
 def expand_kernel(full_ref, gate_ref, up_ref, down_ref, back_hbm, back_ref, leaving):
     hid, width = down_ref.shape
-    capacity = back_ref.shape[1]
-    chunks = leaving.shape[0]
-    rows = full_ref.shape[0] // chunks
-    copies = []
-    for i in range(chunks):
-        full = full_ref[i * rows : (i + 1) * rows, :]
-        outputs = mm(full[:, :hid], down_ref[...]).astype(BF)
-        token_delta = mm(full[:, hid : 2 * hid], gate_ref[...], NT)
-        token_delta = (token_delta + mm(full[:, 2 * hid : 3 * hid], up_ref[...], NT)).astype(BF)
-        mine = pl.ds(i * rows // capacity, rows // capacity)
-        shape = (rows // capacity, capacity, width)
-        back_ref[mine, :, :width] = outputs.reshape(shape)
-        back_ref[mine, :, width : 2 * width] = token_delta.reshape(shape)
-        back_ref[mine, :, 2 * width :] = full[:, 3 * hid :].reshape(shape[:2] + (LANES,))
-        copy = pltpu.make_async_copy(back_ref.at[mine], back_hbm.at[mine], leaving.at[i])
+    experts, capacity, _ = back_ref.shape
+    shape = (experts, capacity, width)
+
+    def send(i, columns):
+        copy = pltpu.make_async_copy(
+            back_ref.at[:, :, columns], back_hbm.at[:, :, columns], leaving.at[i]
+        )
         copy.start()
-        copies.append(copy)
-    for copy in copies:
-        copy.wait()
+        return copy
+
+    outputs = mm(full_ref[:, :hid], down_ref[...]).astype(BF)
+    back_ref[:, :, :width] = outputs.reshape(shape)
+    first = send(0, pl.ds(0, width))
+    token_delta = mm(full_ref[:, hid : 2 * hid], gate_ref[...], NT)
+    token_delta = token_delta + mm(full_ref[:, 2 * hid : 3 * hid], up_ref[...], NT)
+    back_ref[:, :, width : 2 * width] = token_delta.astype(BF).reshape(shape)
+    back_ref[:, :, 2 * width :] = full_ref[:, 3 * hid :].reshape(shape[:2] + (LANES,))
+    second = send(1, pl.ds(width, width + LANES))
+    first.wait()
+    second.wait()
 
 
 def combine_kernel(
@@ -151,39 +171,41 @@
     hid = w_gate.shape[2]
     total = experts * capacity
     part = total // reps
-    gate_mat, up_mat, down_mat = w_gate[0], w_up[0], w_down[0]
 
     ids, weight = expert_ids.T, router_weight.T
-    sent, placing, weighting = pl.pallas_call(
+    sent, placing, weighting, gate_mat, up_mat, down_mat = pl.pallas_call(
         functools.partial(place_kernel, capacity),
         out_shape=(
             jax.ShapeDtypeStruct((experts, capacity, 2 * width), BF),
             jax.ShapeDtypeStruct((total, rows), BF),
             jax.ShapeDtypeStruct((total, rows), BF),
+            jax.ShapeDtypeStruct(w_gate.shape[1:], BF),
+            jax.ShapeDtypeStruct(w_up.shape[1:], BF),
+            jax.ShapeDtypeStruct(w_down.shape[1:], BF),
         ),
         name="place",
-        in_specs=[pl.BlockSpec(memory_space=pltpu.HBM)] * 4,
-        out_specs=(pl.BlockSpec(memory_space=pltpu.VMEM),) * 3,
+        in_specs=[pl.BlockSpec(memory_space=pltpu.HBM)] * 7,
+        out_specs=(pl.BlockSpec(memory_space=pltpu.VMEM),) * 6,
         scratch_shapes=[
             pltpu.VMEM((top, rows), jnp.int32),
             pltpu.VMEM((top, rows), BF),
             pltpu.VMEM((rows, width), BF),
             pltpu.VMEM((rows, width), BF),
-            pltpu.SemaphoreType.DMA((4,)),
+            pltpu.SemaphoreType.DMA((7,)),
         ],
         compiler_params=pltpu.CompilerParams(vmem_limit_bytes=6 * 1024 * 1024),
-    )(*(pltpu.with_memory_space_constraint(a, pltpu.HBM) for a in (ids, weight, tokens, cotangent)))
-    recv = swap(sent, "exp").reshape(total, 2 * width)
+    )(*(pltpu.with_memory_space_constraint(a, pltpu.HBM) for a in (ids, weight, tokens, cotangent, w_gate[0], w_up[0], w_down[0])))
+    recv = swap(sent, "exp")
+    partial = pl.pallas_call(
+        partial_kernel,
+        out_shape=jax.ShapeDtypeStruct((total, 3 * hid), BF),
+        name="partial",
+        in_specs=[pl.BlockSpec(memory_space=pltpu.VMEM)] * 4,
+        out_specs=pl.BlockSpec(memory_space=pltpu.VMEM),
+        compiler_params=pltpu.CompilerParams(vmem_limit_bytes=16 * 1024 * 1024),
+    )(recv, gate_mat, up_mat, down_mat)
+    recv = recv.reshape(total, 2 * width)
     inputs, out_delta = recv[:, :width], recv[:, width:]
-
-    partial = jnp.concatenate(
-        [
-            mm(inputs, gate_mat).astype(BF),
-            mm(inputs, up_mat).astype(BF),
-            mm(out_delta, down_mat, NT).astype(BF),
-        ],
-        axis=1,
-    )
     pieces = swap(partial.reshape(reps, part, 3 * hid), "rep")
     mine = pl.pallas_call(
         activate_kernel,

time: 115 us -> 114 us (level)
    dot_general x6 -> x3, matrix products: 4.99 us -> 3.85 us  [mm(): return lax.dot_general(a, b, dims, preferred_element_type=F32)]
  transfers between devices with their start and end apart: 1 -> 1, of which waited for: 1 -> 1; matrix products, arithmetic and copies ran while one was open for 3% -> 4% of each run, Pallas kernels for 0% -> 0%
where the time goes in v6:
time: 114 us; the launch traced here: 113 us
  blocking collectives  78.3 us (69%)
  waiting for transfers between devices  18 us (16%)
  starting transfers between devices  6.79 us (6%)
  Pallas kernels  5.38 us (5%)
  matrix products  3.85 us (3%)
    all_to_all x3, blocking collectives, swap(): return lax.all_to_all(x, axis, split_axis=0, concat_axis=0, tiled=True)  78.3 us
    all_to_all x1, waiting for transfers between devices, swap(): return lax.all_to_all(x, axis, split_axis=0, concat_axis=0, tiled=True)  18 us
    all_to_all x1, starting transfers between devices, swap(): return lax.all_to_all(x, axis, split_axis=0, concat_axis=0, tiled=True)  6.79 us
    dot_general x3, matrix products, mm(): return lax.dot_general(a, b, dims, preferred_element_type=F32)  3.85 us
  transfers between devices with their start and end apart: 1, of which 1 were waited for; matrix products, arithmetic and copies ran while one was open for 4% of the time, Pallas kernels for 0%

profile of v6, /device:TPU:1, one launch (start us, length us, event | category | flops | bytes accessed | tf_op | source)
XLA Modules:
  0.0 113.2 jit_solution(4466790744697313649)
XLA Ops:
  0.6 1.7 %place.1 = (bf16[128,2,1024]{2,1,0:T(2,128)(2,1)S(1)}, bf16[256,24]{1,0:T(8,128)(2,1)S(1)}, bf16[256,24]{1,0:T(8,128)(2,1)S(1)}, bf16[512,768]{1,0:T(8,128)(2,1)...) custom-call(s32[8,24]{1,0:T(8,128)} %bitcast.19, bf16[8,24]{1,0:T(8,128)(2,1)} %bitcast.21, ...), custom_call_target="tpu_custom_call" | custom-call | tf_op jit(solution)/shard_map/place/pallas_call | solution.py:176
  2.4 38.8 %all_to_all.20.recv_ref = bf16[128,2,1024]{2,1,0:T(2,128)(2,1)S(1)} all-to-all(bf16[128,2,1024]{2,1,0:T(2,128)(2,1)S(1)} %get-tuple-element.17), channel_id=1, replica_groups=mesh['rep'=4,'exp'=128] {'exp'}, dimensions={0} | all-to-all | bytes 1048576 | tf_op jit(solution)/shard_map/all_to_all | solution.py:24
  41.2 0.8 partial.1
  42.0 20.5 %all_to_all.21.pieces_ref = bf16[4,64,2304]{2,1,0:T(8,128)(2,1)S(1)} all-to-all(bf16[4,64,2304]{2,1,0:T(8,128)(2,1)S(1)} %bitcast.18), channel_id=1, replica_groups=mesh['rep'=4,'exp'=128] {'rep'}, dimensions={0} | all-to-all | bytes 2359296 | tf_op jit(solution)/shard_map/all_to_all | solution.py:24
  62.5 0.4 activate.1
  62.9 19.0 %all_to_all.22 = bf16[4,64,2432]{2,1,0:T(8,128)(2,1)S(1)} all-to-all(bf16[4,64,2432]{2,1,0:T(8,128)(2,1)S(1)} %activate.1), channel_id=1, replica_groups=mesh['rep'=4,'exp'=128] {'rep'}, dimensions={0} | all-to-all | bytes 2490368 | tf_op jit(solution)/shard_map/all_to_all | solution.py:24
  81.8 1.5 %expand.1 = bf16[128,2,1152]{2,1,0:T(2,128)(2,1)} custom-call(bf16[256,2432]{1,0:T(8,128)(2,1)S(1)} %bitcast.14, bf16[512,768]{1,0:T(8,128)(2,1)S(1)} %get-tuple-element.18.gate_ref, bf16[512,768]{1,0:T(8,128)(2,1)S(1)} %get-tuple-element.19.up_ref, bf16[768,512]{1,0:T(8,128)(2,1)S(1)} %get-tuple-element.20.down_ref), custom_call_target="tpu_custom_call" | custom-call | tf_op jit(solution)/shard_map/expand/pallas_call | solution.py:223
  83.4 6.8 %all-to-all-start.3 = ((bf16[128,2,1152]{2,1,0:T(2,128)(2,1)}), bf16[128,2,1152]{2,1,0:T(2,128)(2,1)S(1)}, u32[]{:S(2)}, u32[]{:S(2)}) async-start(bf16[128,2,1152]{2,1,0:T(2,128)(2,1)} %expand.1), calls=%async_computation.3 | async-start | bytes 1179648 | tf_op jit(solution)/shard_map/all_to_all | solution.py:24
  90.2 0.2 reshape.23
  90.4 1.3 %fusion.1 = bf16[1,512,768]{2,1,0:T(8,128)(2,1)} fusion(bf16[256,2432]{1,0:T(8,128)(2,1)S(1)} %bitcast.15, bf16[256,1024]{1,0:T(8,128)(2,1)S(1)} %reshape.23), kind=kOutput, calls=%fused_computation.4 | convolution fusion | flops 201719808 | bytes 1441792 | tf_op jit(solution)/shard_map/dot_general | solution.py:16
  91.7 0.0 copy-start
  91.7 0.0 copy-start.1
  91.7 1.3 %fusion = bf16[1,512,768]{2,1,0:T(8,128)(2,1)} fusion(bf16[256,2432]{1,0:T(8,128)(2,1)S(1)} %bitcast.16, bf16[256,1024]{1,0:T(8,128)(2,1)S(1)} %reshape.23), kind=kOutput, calls=%fused_computation.3 | convolution fusion | flops 201719808 | bytes 1441792 | tf_op jit(solution)/shard_map/dot_general | solution.py:16
  93.0 1.3 %fusion.2 = bf16[1,768,512]{2,1,0:T(8,128)(2,1)} fusion(bf16[256,2432]{1,0:T(8,128)(2,1)S(1)} %bitcast.17, bf16[256,1024]{1,0:T(8,128)(2,1)S(1)} %reshape.23), kind=kOutput, calls=%fused_computation.5 | convolution fusion | flops 201719808 | bytes 1441792 | tf_op jit(solution)/shard_map/dot_general | solution.py:16
  94.2 18.0 %all-to-all-done.3.back_ref = bf16[128,2,1152]{2,1,0:T(2,128)(2,1)S(1)} async-done(((bf16[128,2,1152]{2,1,0:T(2,128)(2,1)}), bf16[128,2,1152]{2,1,0:T(2,128)(2,1)S(1)}, u32[]{:S(2)}, u32[]{:S(2)}) %all-to-all-start.3) | async-done | bytes 589856 | tf_op jit(solution)/shard_map/all_to_all | solution.py:24
  112.2 0.0 copy-done
  112.2 0.0 copy-done.1
  112.3 1.0 combine.1
Async XLA Ops:
  83.4 28.9 %all-to-all-start.3 = ((bf16[128,2,1152]{2,1,0:T(2,128)(2,1)}), bf16[128,2,1152]{2,1,0:T(2,128)(2,1)S(1)}, u32[]{:S(2)}, u32[]{:S(2)}) async-start(bf16[128,2,1152]{2,1,0:T(2,128)(2,1)} %expand.1), calls=%async_computation.3 | async-start | bytes 1179648 | tf_op jit(solution)/shard_map/all_to_all | solution.py:24
  91.7 20.6 %copy-start = (s32[24,8]{0,1:T(8,128)S(1)}, s32[24,8]{0,1:T(8,128)}, u32[]{:S(2)}) copy-start(s32[24,8]{0,1:T(8,128)} %param.10) | copy-start | bytes 2308
  91.7 20.6 %copy-start.1 = (bf16[24,8]{0,1:T(8,128)(2,1)S(1)}, bf16[24,8]{0,1:T(8,128)(2,1)}, u32[]{:S(2)}) copy-start(bf16[24,8]{0,1:T(8,128)(2,1)} %param.9) | copy-start | bytes 1156

commit v7 on v6

--- a/solution.py
+++ b/solution.py
@@ -119,39 +119,62 @@
         mine_ref[r, :, 3 * hid :] = scaled
 
 
-def expand_kernel(full_ref, gate_ref, up_ref, down_ref, back_hbm, back_ref, leaving):
+def expand_kernel(full_ref, gate_ref, up_ref, down_ref, back_ref):
     hid, width = down_ref.shape
     experts, capacity, _ = back_ref.shape
     shape = (experts, capacity, width)
-
-    def send(i, columns):
-        copy = pltpu.make_async_copy(
-            back_ref.at[:, :, columns], back_hbm.at[:, :, columns], leaving.at[i]
-        )
-        copy.start()
-        return copy
-
     outputs = mm(full_ref[:, :hid], down_ref[...]).astype(BF)
     back_ref[:, :, :width] = outputs.reshape(shape)
-    first = send(0, pl.ds(0, width))
     token_delta = mm(full_ref[:, hid : 2 * hid], gate_ref[...], NT)
     token_delta = token_delta + mm(full_ref[:, 2 * hid : 3 * hid], up_ref[...], NT)
     back_ref[:, :, width : 2 * width] = token_delta.astype(BF).reshape(shape)
     back_ref[:, :, 2 * width :] = full_ref[:, 3 * hid :].reshape(shape[:2] + (LANES,))
-    second = send(1, pl.ds(width, width + LANES))
-    first.wait()
-    second.wait()
-
-
-def combine_kernel(
-    capacity, ids_ref, weight_ref, placing_ref, weighting_ref, back_ref, mixed_ref, grad_ref, router_ref
+
+
+def finish_kernel(
+    capacity,
+    ids_ref,
+    weight_ref,
+    placing_ref,
+    weighting_ref,
+    full_ref,
+    recv_ref,
+    back_ref,
+    mixed_hbm,
+    grad_hbm,
+    router_hbm,
+    gate_hbm,
+    up_hbm,
+    down_hbm,
+    mixed_ref,
+    grad_ref,
+    router_ref,
+    gate_ref,
+    up_ref,
+    down_ref,
+    leaving,
 ):
     top, rows = ids_ref.shape
     total = placing_ref.shape[0]
     width = mixed_ref.shape[1]
-    back = back_ref[...].reshape(total, back_ref.shape[2])
-    mixed_ref[...] = mm(weighting_ref[...], back[:, :width], TN).astype(BF)
-    grad_ref[...] = mm(placing_ref[...], back[:, width : 2 * width], TN).astype(BF)
+    hid = gate_ref.shape[1]
+    inputs = recv_ref[:, :, :width].reshape(total, width)
+    out_delta = recv_ref[:, :, width:].reshape(total, width)
+    copies = []
+
+    def send(value, buffer, target):
+        buffer[...] = value.astype(BF)
+        copy = pltpu.make_async_copy(buffer, target, leaving.at[len(copies)])
+        copy.start()
+        copies.append(copy)
+
+    send(mm(full_ref[:, :hid].T, out_delta), down_ref, down_hbm)
+    inputs = inputs.T
+    send(mm(inputs, full_ref[:, hid : 2 * hid]), gate_ref, gate_hbm)
+    send(mm(inputs, full_ref[:, 2 * hid : 3 * hid]), up_ref, up_hbm)
+    back = back_ref[...]
+    send(mm(weighting_ref[...], back[:, :width], TN), mixed_ref, mixed_hbm)
+    send(mm(placing_ref[...], back[:, width : 2 * width], TN), grad_ref, grad_hbm)
     expert = lax.broadcasted_iota(jnp.int32, (total, rows), 0) // capacity
     routed = back[:, 2 * width :].astype(F32)[:, :rows] * placing_ref[...].astype(F32)
     sums = [
@@ -159,7 +182,9 @@
         for k in range(top)
     ]
     sums = jnp.concatenate(sums, axis=0) / weight_ref[...].astype(F32)
-    router_ref[...] = sums.astype(BF)
+    send(sums, router_ref, router_hbm)
+    for copy in copies:
+        copy.wait()
 
 
 def local(tokens, cotangent, router_weight, expert_ids, w_gate, w_up, w_down):
@@ -204,8 +229,6 @@
         out_specs=pl.BlockSpec(memory_space=pltpu.VMEM),
         compiler_params=pltpu.CompilerParams(vmem_limit_bytes=16 * 1024 * 1024),
     )(recv, gate_mat, up_mat, down_mat)
-    recv = recv.reshape(total, 2 * width)
-    inputs, out_delta = recv[:, :width], recv[:, width:]
     pieces = swap(partial.reshape(reps, part, 3 * hid), "rep")
     mine = pl.pallas_call(
         activate_kernel,
@@ -216,37 +239,35 @@
         compiler_params=pltpu.CompilerParams(vmem_limit_bytes=8 * 1024 * 1024),
     )(pieces)
     full = swap(mine, "rep").reshape(total, -1)
-    hidden, gate_delta = full[:, :hid], full[:, hid : 2 * hid]
-    up_delta = full[:, 2 * hid : 3 * hid]
-
     shape = (experts, capacity, 2 * width + LANES)
     back = pl.pallas_call(
         expand_kernel,
         out_shape=jax.ShapeDtypeStruct(shape, BF),
         name="expand",
         in_specs=[pl.BlockSpec(memory_space=pltpu.VMEM)] * 4,
-        out_specs=pl.BlockSpec(memory_space=pltpu.HBM),
-        scratch_shapes=[pltpu.VMEM(shape, BF), pltpu.SemaphoreType.DMA((2,))],
+        out_specs=pl.BlockSpec(memory_space=pltpu.VMEM),
         compiler_params=pltpu.CompilerParams(vmem_limit_bytes=12 * 1024 * 1024),
     )(full, gate_mat, up_mat, down_mat)
     back = swap(back, "exp")
 
-    down_grad = mm(hidden, out_delta, TN).astype(BF)
-    gate_grad = mm(inputs, gate_delta, TN).astype(BF)
-    up_grad = mm(inputs, up_delta, TN).astype(BF)
-
-    mixed, token_grad, router_grad = pl.pallas_call(
-        functools.partial(combine_kernel, capacity),
+    vmem, hbm = pl.BlockSpec(memory_space=pltpu.VMEM), pl.BlockSpec(memory_space=pltpu.HBM)
+    grads = [(width, hid), (width, hid), (hid, width)]
+    small = [(rows, width), (rows, width), (top, rows)]
+    mixed, token_grad, router_grad, gate_grad, up_grad, down_grad = pl.pallas_call(
+        functools.partial(finish_kernel, capacity),
         out_shape=(
             jax.ShapeDtypeStruct((rows, width), BF),
             jax.ShapeDtypeStruct((rows, width), BF),
             jax.ShapeDtypeStruct((top, rows), BF),
-        ),
-        name="combine",
-        in_specs=[pl.BlockSpec(memory_space=pltpu.VMEM)] * 5,
-        out_specs=(pl.BlockSpec(memory_space=pltpu.VMEM),) * 3,
-        compiler_params=pltpu.CompilerParams(vmem_limit_bytes=6 * 1024 * 1024),
-    )(ids, weight, placing, weighting, back)
+        )
+        + tuple(jax.ShapeDtypeStruct(g, BF) for g in grads),
+        name="finish",
+        in_specs=[vmem] * 7,
+        out_specs=(hbm,) * 6,
+        scratch_shapes=[pltpu.VMEM(g, BF) for g in small + grads]
+        + [pltpu.SemaphoreType.DMA((6,))],
+        compiler_params=pltpu.CompilerParams(vmem_limit_bytes=24 * 1024 * 1024),
+    )(ids, weight, placing, weighting, full, recv, back.reshape(total, -1))
     router_grad = router_grad.T
     return (mixed, token_grad, router_grad, gate_grad[None], up_grad[None], down_grad[None])
 

time: 114 us -> 113 us (level)
  blocking collectives: 78.3 us -> 107 us
  waiting for transfers between devices: 18 us -> 0 us
  starting transfers between devices: 6.79 us -> 0 us
  matrix products: 3.85 us -> 0 us
    all_to_all x3 -> x4, blocking collectives: 78.3 us -> 107 us  [swap(): return lax.all_to_all(x, axis, split_axis=0, concat_axis=0, tiled=True)]
    all_to_all x1 -> x0, waiting for transfers between devices: 18 us -> none  [swap(): return lax.all_to_all(x, axis, split_axis=0, concat_axis=0, tiled=True)]
    all_to_all x1 -> x0, starting transfers between devices: 6.79 us -> none  [swap(): return lax.all_to_all(x, axis, split_axis=0, concat_axis=0, tiled=True)]
    dot_general x3 -> x0, matrix products: 3.85 us -> none  [mm(): return lax.dot_general(a, b, dims, preferred_element_type=F32)]
  transfers between devices with their start and end apart: 1 -> 0, of which waited for: 1 -> 0; matrix products, arithmetic and copies ran while one was open for 4% -> 0% of each run, Pallas kernels for 0% -> 0%
where the time goes in v7:
time: 113 us
  blocking collectives  107 us (95%)
  Pallas kernels  5.71 us (5%)
    all_to_all x4, blocking collectives, swap(): return lax.all_to_all(x, axis, split_axis=0, concat_axis=0, tiled=True)  107 us

profile of v7, /device:TPU:1, one launch (start us, length us, event | category | flops | bytes accessed | tf_op | source)
XLA Modules:
  0.0 113.2 jit_solution(16368170230715527059)
XLA Ops:
  0.6 1.7 %place.1 = (bf16[128,2,1024]{2,1,0:T(2,128)(2,1)S(1)}, bf16[256,24]{1,0:T(8,128)(2,1)S(1)}, bf16[256,24]{1,0:T(8,128)(2,1)S(1)}, bf16[512,768]{1,0:T(8,128)(2,1)...) custom-call(s32[8,24]{1,0:T(8,128)} %bitcast.14, bf16[8,24]{1,0:T(8,128)(2,1)} %bitcast.16, ...), custom_call_target="tpu_custom_call" | custom-call | tf_op jit(solution)/shard_map/place/pallas_call | solution.py:201
  2.4 38.8 %all_to_all.20.recv_ref = bf16[128,2,1024]{2,1,0:T(2,128)(2,1)S(1)} all-to-all(bf16[128,2,1024]{2,1,0:T(2,128)(2,1)S(1)} %get-tuple-element.20), channel_id=1, replica_groups=mesh['rep'=4,'exp'=128] {'exp'}, dimensions={0} | all-to-all | bytes 1048576 | tf_op jit(solution)/shard_map/all_to_all | solution.py:24
  41.2 0.8 partial.1
  42.0 20.5 %all_to_all.21.pieces_ref = bf16[4,64,2304]{2,1,0:T(8,128)(2,1)S(1)} all-to-all(bf16[4,64,2304]{2,1,0:T(8,128)(2,1)S(1)} %bitcast.13), channel_id=1, replica_groups=mesh['rep'=4,'exp'=128] {'rep'}, dimensions={0} | all-to-all | bytes 2359296 | tf_op jit(solution)/shard_map/all_to_all | solution.py:24
  62.5 0.4 activate.1
  62.9 19.0 %all_to_all.22 = bf16[4,64,2432]{2,1,0:T(8,128)(2,1)S(1)} all-to-all(bf16[4,64,2432]{2,1,0:T(8,128)(2,1)S(1)} %activate.1), channel_id=1, replica_groups=mesh['rep'=4,'exp'=128] {'rep'}, dimensions={0} | all-to-all | bytes 2490368 | tf_op jit(solution)/shard_map/all_to_all | solution.py:24
  81.8 0.8 expand.1
  82.6 0.0 copy-start
  82.6 0.0 copy-start.1
  82.7 28.2 %all_to_all.23 = bf16[128,2,1152]{2,1,0:T(2,128)(2,1)S(1)} all-to-all(bf16[128,2,1152]{2,1,0:T(2,128)(2,1)S(1)} %expand.1), channel_id=1, replica_groups=mesh['rep'=4,'exp'=128] {'exp'}, dimensions={0} | all-to-all | bytes 1179648 | tf_op jit(solution)/shard_map/all_to_all | solution.py:24
  110.9 0.2 reshape.23.back_ref
  111.1 0.0 copy-done
  111.1 0.0 copy-done.1
  111.1 2.0 %finish.1 = (bf16[24,512]{1,0:T(8,128)(2,1)}, bf16[24,512]{1,0:T(8,128)(2,1)}, bf16[8,24]{1,0:T(8,128)(2,1)}, bf16[512,768]{1,0:T(8,128)(2,1)}, bf16[512,768]{1,0:T(8,128)(2,1)}, /*index=5*/bf16[768,512]{1,0:T(8,128)(2,1)}) custom-call(s32[8,24]{1,0:T(8,128)S(1)} %bitcast.15, bf16[8,24]{1,0:T(8,128)(2,1)S(1)} %bitcast.17, ...), custom_call_target="tpu_custom_call" | custom-call | tf_op jit(solution)/shard_map/finish/pallas_call | solution.py:256
Async XLA Ops:
  82.6 28.5 %copy-start = (s32[24,8]{0,1:T(8,128)S(1)}, s32[24,8]{0,1:T(8,128)}, u32[]{:S(2)}) copy-start(s32[24,8]{0,1:T(8,128)} %param.10) | copy-start | bytes 2308
  82.6 28.5 %copy-start.1 = (bf16[24,8]{0,1:T(8,128)(2,1)S(1)}, bf16[24,8]{0,1:T(8,128)(2,1)}, u32[]{:S(2)}) copy-start(bf16[24,8]{0,1:T(8,128)(2,1)} %param.9) | copy-start | bytes 1156
